TPU v7x, 32 devices: a whole 2x2x4 slice. The times are simulated.
32 devices in a mesh: groups: 2 (over y), frame: 8 (over z, x), row: 2 (over core).
Axes of the slice: x: 2, y: 2, z: 4, core: 2. Of those that a mesh axis runs over, the one named last changes fastest.
Arguments:
- latents: bfloat16 [16, 1024, 256], P(('groups', 'frame'), 'row'), parts along dimension 0, may hold values from -8 to 8
- ref_frames: int32 [16, 2], P(('groups', 'frame')), parts along dimension 0, may hold values from 0 to 7, as said below
- windows: int32 [16], P(('groups', 'frame')), parts along dimension 0, may hold values from 1 to 2, as said below
- quant_level: int32 [16], P(('groups', 'frame')), parts along dimension 0, may hold values from 0 to 63
- quant_scale: float32 [64, 256], replicated, may hold values from 0.5 to 2
- shared_proj: bfloat16 [256, 256], replicated, may hold values from -0.375 to 0.375
- value_proj: bfloat16 [256, 256], replicated, may hold values from -0.375 to 0.375
- output_proj: bfloat16 [256, 256], replicated, may hold values from -0.75 to 0.75
- conv_taps: bfloat16 [3, 256, 256], replicated, may hold values from -0.21875 to 0.21875
- cotangent: bfloat16 [16, 1024, 256], P(('groups', 'frame'), 'row'), parts along dimension 0, may hold values from -6 to 6
Outputs:
- coded_latent: bfloat16 [16, 1024, 256], P(('groups', 'frame'), 'row'), parts along dimension 0
- grad_latents: bfloat16 [16, 1024, 256], P(('groups', 'frame'), 'row'), parts along dimension 0
- grad_shared: float32 [512, 256], P('groups'), parts along dimension 0
- grad_values: float32 [512, 256], P('groups'), parts along dimension 0
- grad_output: float32 [512, 256], P('groups'), parts along dimension 0
- grad_taps: float32 [6, 256, 256], P('groups'), parts along dimension 0
There are 2 independent parts, one for each index of `groups`. A program takes and returns all parts, laid end to end along the dimension named above; an argument that names none is the same for every part. Nothing has to cross between parts.
Inputs may be any that keep to these rules, and one draw needn't show every extreme that they name: ref_frames[f, s] differs from f by a power of two no larger than 2 ** 2, and that largest distance occurs. `windows`: some frame has a window of 2 rows.
All inputs are finite; a program needn't handle non-finite values.
Results may differ from a plain program's by a relative error of at most 0.0045.
The roundings to bfloat16 on the way count: a program that leaves them out, or rounds other values in their place, can miss the bound.
Values may be sent and summed in bfloat16 or wider, within the bound.
A program may use at most 128 MiB of HBM per device.

v0:
```python
import functools
import math

import jax
import jax.numpy as jnp
from jax import lax
from jax.experimental import pallas as pl
from jax.experimental.pallas import tpu as pltpu
from jax.sharding import PartitionSpec as P

HEADS = 8
DH = 32
COLS = 64
QBLK = 4
WMAX = 2

SCORE_SCALE = 1.5 / math.sqrt(DH)
LOG2E = math.log2(math.e)
BF = jnp.bfloat16
F32 = jnp.float32


def mm(a, b, ca=1, cb=0):
    return lax.dot_general(a, b, (((ca,), (cb,)), ((), ())), preferred_element_type=F32)


def attention_kernel(
    meta_ref, buf_hbm, halo_hbm, x_hbm, q_hbm, qt_hbm, do_hbm, dot_hbm, resid_hbm,
    sp_ref, vp_ref, op_ref,
    residual_ref, hidden_ref, base_ref, part_ref, gs_ref, gv_ref, go_ref,
    xs_ref, k_ref, v_ref, kt_ref, vt_ref, mixt_ref, dqt_ref, dk_ref, dv_ref,
    s_scr, dp_scr, p_scr, ds_scr, qm_scr, dom_scr,
    x_ref, q_ref, qt_ref, do_ref, dot_ref, resid_ref, sems,
):
    tokens, width = q_ref.shape
    nq = QBLK * COLS
    span = (QBLK + 2 * WMAX) * COLS
    rows = span // COLS
    blocks = tokens // nq
    half = width // 2
    per_half = HEADS // 2
    lane = lax.broadcasted_iota(jnp.int32, (1, width), 1) // DH
    sub = lax.broadcasted_iota(jnp.int32, (half, 1), 0) // DH

    dk_ref[...] = jnp.zeros_like(dk_ref)
    dv_ref[...] = jnp.zeros_like(dv_ref)
    rim = WMAX * COLS
    window = meta_ref[2]
    row_id = meta_ref[3]
    first_row = row_id * (tokens // COLS)
    total_rows = meta_ref[4]
    bottom = rim + tokens
    held = pl.multiple_of(jnp.where(row_id == 0, bottom, 0), rim)
    empty = pl.multiple_of(jnp.where(row_id == 0, 0, bottom), rim)
    moves = []
    for s in range(2):
        kind = meta_ref[s]
        moves.append((buf_hbm.at[kind], xs_ref.at[s, pl.ds(rim, tokens)]))
        moves.append((halo_hbm.at[kind], xs_ref.at[s, pl.ds(held, rim)]))
    moves += [
        (q_hbm, q_ref), (do_hbm, do_ref), (qt_hbm, qt_ref), (dot_hbm, dot_ref),
        (x_hbm, x_ref), (resid_hbm, resid_ref),
    ]
    copies = [
        pltpu.make_async_copy(source, target, sems.at[i])
        for i, (source, target) in enumerate(moves)
    ]
    for move in copies:
        move.start()
    for s in range(2):
        xs_ref[s, pl.ds(empty, rim), :] = jnp.zeros((rim, width), BF)
        copies[2 * s].wait()
        copies[2 * s + 1].wait()
        xs = xs_ref[s]
        keys = mm(xs, sp_ref[...]).astype(BF)
        vals = mm(xs, vp_ref[...]).astype(BF)
        k_ref[s] = keys
        v_ref[s] = vals
        kt_ref[s] = keys.T
        vt_ref[s] = vals.T
    for move in copies[4:]:
        move.wait()
    query_row = lax.broadcasted_iota(jnp.int32, (1, nq), 1) // COLS

    def bias_row(b, c):
        key_row = first_row + b * QBLK + c - WMAX
        reach = jnp.where((key_row >= 0) & (key_row < total_rows), window, -1)
        return jnp.where(jnp.abs(c - WMAX - query_row) <= reach, 0.0, -jnp.inf).astype(F32)

    for b in range(blocks):
        q0 = b * nq
        qb = q_ref[q0 : q0 + nq, :]
        dob = do_ref[q0 : q0 + nq, :]
        for h in range(HEADS):
            keep = lane == h
            qm_scr[h * nq : (h + 1) * nq, :] = jnp.where(keep, qb, jnp.zeros_like(qb))
            dom_scr[h * nq : (h + 1) * nq, :] = jnp.where(keep, dob, jnp.zeros_like(dob))

        for hf in range(2):
            f0 = hf * half
            qth = qt_ref[f0 : f0 + half, q0 : q0 + nq]
            doth = dot_ref[f0 : f0 + half, q0 : q0 + nq]

            def one_head(hh, carry, hf=hf, f0=f0, qth=qth, doth=doth, q0=q0, b=b):
                keep = sub == hh
                qtm = jnp.where(keep, qth, jnp.zeros_like(qth))
                dotm = jnp.where(keep, doth, jnp.zeros_like(doth))
                for s in range(2):
                    s_scr[s * span : (s + 1) * span, :] = mm(
                        k_ref[s, q0 : q0 + span, f0 : f0 + half], qtm
                    )
                    dp_scr[s * span : (s + 1) * span, :] = mm(
                        v_ref[s, q0 : q0 + span, f0 : f0 + half], dotm
                    )
                m8 = jnp.full((8, nq), -jnp.inf, F32)
                for c in range(2 * rows):
                    x = s_scr[c * COLS : (c + 1) * COLS, :].reshape(COLS // 8, 8, nq)
                    m8 = jnp.maximum(m8, jnp.max(x, axis=0) + bias_row(b, c % rows))
                m = jnp.max(m8, axis=0, keepdims=True)
                kk = SCORE_SCALE * LOG2E
                l8 = jnp.zeros((8, nq), F32)
                u8 = jnp.zeros((8, nq), F32)
                for c in range(2 * rows):
                    sl = slice(c * COLS, (c + 1) * COLS)
                    off = (bias_row(b, c % rows) - m) * kk
                    p = jnp.exp2(s_scr[sl, :] * kk + off)
                    s_scr[sl, :] = p
                    l8 = l8 + jnp.sum(p.reshape(COLS // 8, 8, nq), axis=0)
                    u8 = u8 + jnp.sum((p * dp_scr[sl, :]).reshape(COLS // 8, 8, nq), axis=0)
                inv = 1.0 / jnp.sum(l8, axis=0, keepdims=True)
                ci = inv * SCORE_SCALE
                inner = jnp.sum(u8, axis=0, keepdims=True) * inv * ci
                col = pl.multiple_of((hf * per_half + hh) * nq, nq)
                for c in range(2 * rows):
                    sl = slice(c * COLS, (c + 1) * COLS)
                    p = s_scr[sl, :]
                    p_scr[sl, pl.ds(col, nq)] = (p * inv).astype(BF)
                    ds_scr[sl, pl.ds(col, nq)] = (p * (dp_scr[sl, :] * ci - inner)).astype(BF)
                r0 = pl.multiple_of(f0 + hh * DH, DH)
                mix = jnp.zeros((DH, nq), F32)
                dq = jnp.zeros((DH, nq), F32)
                for s in range(2):
                    ks = slice(s * span, (s + 1) * span)
                    mix = mix + mm(
                        vt_ref[s, pl.ds(r0, DH), q0 : q0 + span], p_scr[ks, pl.ds(col, nq)]
                    )
                    dq = dq + mm(
                        kt_ref[s, pl.ds(r0, DH), q0 : q0 + span], ds_scr[ks, pl.ds(col, nq)]
                    )
                mixt_ref[pl.ds(r0, DH), q0 : q0 + nq] = mix.astype(BF)
                dqt_ref[pl.ds(r0, DH), q0 : q0 + nq] = dq
                return carry

            lax.fori_loop(0, per_half, one_head, 0)

        for s in range(2):
            ks = slice(s * span, (s + 1) * span)
            dk_ref[s, q0 : q0 + span, :] += mm(ds_scr[ks, :], qm_scr[...])
            dv_ref[s, q0 : q0 + span, :] += mm(p_scr[ks, :], dom_scr[...])

    dq = dqt_ref[...].T.astype(BF)
    base_ref[...] = resid_ref[...] + mm(dq, sp_ref[...], 1, 1)
    mixt = mixt_ref[...]
    go_ref[...] = mm(mixt, resid_ref[...].astype(BF))
    residual = x_ref[...].astype(F32) + mm(mixt.T, op_ref[...])
    residual_ref[...] = residual
    hidden_ref[...] = residual.astype(BF)
    gs = mm(x_ref[...].T, dq)
    gv = jnp.zeros((width, width), F32)
    for s in range(2):
        dk = dk_ref[s].astype(BF)
        dv = dv_ref[s].astype(BF)
        part_ref[s] = mm(dk, sp_ref[...], 1, 1) + mm(dv, vp_ref[...], 1, 1)
        xst = xs_ref[s].T
        gs = gs + mm(xst, dk)
        gv = gv + mm(xst, dv)
    gs_ref[...] = gs
    gv_ref[...] = gv


def attention(meta, buf, halo, x, q, qt, do, dot, resid, shared, value, output):
    tokens, width = q.shape
    ext = tokens + 2 * WMAX * COLS
    nq = QBLK * COLS
    keys = 2 * (QBLK + 2 * WMAX) * COLS
    vm = pl.BlockSpec(memory_space=pltpu.VMEM)
    full = jax.ShapeDtypeStruct((tokens, width), F32)
    square = jax.ShapeDtypeStruct((width, width), F32)
    return pl.pallas_call(
        attention_kernel,
        out_shape=(
            full,
            jax.ShapeDtypeStruct((tokens, width), BF),
            full,
            jax.ShapeDtypeStruct((2, ext, width), F32),
            square, square, square,
        ),
        in_specs=[pl.BlockSpec(memory_space=pltpu.SMEM)]
        + [pl.BlockSpec(memory_space=pltpu.MemorySpace.HBM)] * 8
        + [vm] * 3,
        out_specs=(vm,) * 7,
        scratch_shapes=[
            pltpu.VMEM((2, ext, width), BF),
            pltpu.VMEM((2, ext, width), BF),
            pltpu.VMEM((2, ext, width), BF),
            pltpu.VMEM((2, width, ext), BF),
            pltpu.VMEM((2, width, ext), BF),
            pltpu.VMEM((width, tokens), BF),
            pltpu.VMEM((width, tokens), F32),
            pltpu.VMEM((2, ext, width), F32),
            pltpu.VMEM((2, ext, width), F32),
            pltpu.VMEM((keys, nq), F32),
            pltpu.VMEM((keys, nq), F32),
            pltpu.VMEM((keys, HEADS * nq), BF),
            pltpu.VMEM((keys, HEADS * nq), BF),
            pltpu.VMEM((HEADS * nq, width), BF),
            pltpu.VMEM((HEADS * nq, width), BF),
            pltpu.VMEM((tokens, width), BF),
            pltpu.VMEM((tokens, width), BF),
            pltpu.VMEM((width, tokens), BF),
            pltpu.VMEM((tokens, width), BF),
            pltpu.VMEM((width, tokens), BF),
            pltpu.VMEM((tokens, width), F32),
            pltpu.SemaphoreType.DMA((10,)),
        ],
        compiler_params=pltpu.CompilerParams(vmem_limit_bytes=66_000_000),
        cost_estimate=pl.CostEstimate(
            flops=int(2e10), bytes_accessed=int(8e6), transcendentals=int(4e6)
        ),
        name="attention",
    )(meta, buf, halo, x, q, qt, do, dot, resid, shared, value, output)


MESH = pl.DeviceIdType.MESH
CHUNKS = 4


def greet(targets):
    barrier = pltpu.get_barrier_semaphore()
    count = 0
    for exists, device in targets:

        @pl.when(exists)
        def _(device=device):
            pl.semaphore_signal(barrier, inc=1, device_id=device, device_id_type=MESH)

        count = count + jnp.where(exists, 1, 0)
    pl.semaphore_wait(barrier, count)


def fetch_kernel(
    frames, level_ref, x_ref, ct_ref, qs_ref, sp_ref, op_ref, taps_ref,
    buf_ref, halo_ref, q_ref, qt_ref, do_ref, dot_ref, gzb_ref, resid_ref, gain_ref,
    cth_ref, ext_ref, ssem, rsem, hs, hr, cs, cr,
):
    f = lax.axis_index("frame")
    r = lax.axis_index("row")
    tokens = x_ref.shape[0]
    odd = lax.rem(f, 2)
    pair = f + 1 - 2 * odd
    lo2, hi2, lo4, hi4 = f >= 2, f + 2 < frames, f >= 4, f + 4 < frames
    side = ((odd == 1) & (f + 1 < frames)) | ((odd == 0) & (f >= 1))
    always = f >= 0
    have = (lo2, hi2, always, lo4, hi4, side)
    partner = {"row": 1 - r}
    up, down, across = {"frame": f + 2}, {"frame": f - 2}, {"frame": pair}
    greet(((hi2, up), (lo2, down), (always, across), (always, partner)))

    edge = ct_ref.shape[0] - COLS
    ct_copy = pltpu.make_async_remote_copy(
        ct_ref.at[pl.ds(pl.multiple_of((1 - r) * edge, COLS), COLS)], cth_ref, cs, cr,
        device_id=partner, device_id_type=MESH,
    )
    ct_copy.start()
    step = tokens // CHUNKS

    def copy(kind, c, source, device):
        part = pl.ds(c * step, step)
        return pltpu.make_async_remote_copy(
            source.at[part], buf_ref.at[kind, part], ssem.at[kind, c], rsem.at[kind, c],
            device_id=device, device_id_type=MESH,
        )

    for c in range(CHUNKS):

        @pl.when(hi2)
        def _():
            copy(0, c, x_ref, up).start()

        @pl.when(lo2)
        def _():
            copy(1, c, x_ref, down).start()

        copy(2, c, x_ref, across).start()

    for c in range(CHUNKS):

        @pl.when(lo2)
        def _():
            copy(0, c, x_ref, across).wait_recv()

        @pl.when(lo2 & hi2)
        def _():
            copy(3, c, buf_ref.at[0], up).start()

        @pl.when(lo2 & (odd == 1))
        def _():
            copy(5, c, buf_ref.at[0], across).start()

        @pl.when(hi2)
        def _():
            copy(1, c, x_ref, across).wait_recv()

        @pl.when(hi2 & lo2)
        def _():
            copy(4, c, buf_ref.at[1], down).start()

        @pl.when(hi2 & (odd == 0))
        def _():
            copy(5, c, buf_ref.at[1], across).start()

    level = lax.broadcasted_iota(jnp.int32, (qs_ref.shape[0], 1), 0)
    gain = jnp.sum(
        jnp.where(level == level_ref[0], qs_ref[...], 0.0), axis=0, keepdims=True
    )
    gain_ref[...] = gain
    queries = mm(x_ref[...], sp_ref[...]).astype(BF)
    q_ref[...] = queries
    qt_ref[...] = queries.T
    grad_z = ct_ref[...].astype(F32) * gain
    grad_zb = grad_z.astype(BF)
    gzb_ref[...] = grad_zb
    ct_copy.wait()
    outer = (cth_ref[...].astype(F32) * gain).astype(BF)
    blank = jnp.zeros_like(outer)
    ext_ref[COLS : COLS + tokens, :] = grad_zb

    @pl.when(r == 0)
    def _():
        ext_ref[:COLS, :] = blank
        ext_ref[COLS + tokens :, :] = outer

    @pl.when(r != 0)
    def _():
        ext_ref[:COLS, :] = outer
        ext_ref[COLS + tokens :, :] = blank

    resid = grad_z
    for t in range(3):
        resid = resid + mm(ext_ref[(2 - t) * COLS : (2 - t) * COLS + tokens, :], taps_ref[t], 1, 1)
    resid_ref[...] = resid
    grad_mixed = mm(resid.astype(BF), op_ref[...], 1, 1).astype(BF)
    do_ref[...] = grad_mixed
    dot_ref[...] = grad_mixed.T

    rim = WMAX * COLS
    start = pl.multiple_of((1 - r) * (tokens - rim), rim)

    def halo(kind):
        return pltpu.make_async_remote_copy(
            buf_ref.at[kind, pl.ds(start, rim)], halo_ref.at[kind], hs.at[kind], hr.at[kind],
            device_id=partner, device_id_type=MESH,
        )

    for kind in range(6):

        @pl.when(have[kind])
        def _():
            if kind > 1:
                for c in range(CHUNKS):
                    copy(kind, c, x_ref, across).wait_recv()
            halo(kind).start()

    sent = (hi2, lo2, always, lo2 & hi2, lo2 & hi2, (lo2 & (odd == 1)) | (hi2 & (odd == 0)))
    for kind in range(6):

        @pl.when(have[kind])
        def _():
            halo(kind).wait()

        @pl.when(sent[kind])
        def _():
            for c in range(CHUNKS):
                copy(kind, c, x_ref, across).wait_send()


def fetch(level, tokens, cotangent, scale, shared, output, taps, frames):
    count, width = tokens.shape
    vm = pl.BlockSpec(memory_space=pltpu.VMEM)
    dma = pltpu.SemaphoreType.DMA
    rows = jax.ShapeDtypeStruct((count, width), BF)
    columns = jax.ShapeDtypeStruct((width, count), BF)
    return pl.pallas_call(
        functools.partial(fetch_kernel, frames),
        out_shape=(
            jax.ShapeDtypeStruct((6, count, width), BF),
            jax.ShapeDtypeStruct((6, WMAX * COLS, width), BF),
            rows, columns, rows, columns, rows,
            jax.ShapeDtypeStruct((count, width), F32),
            jax.ShapeDtypeStruct((1, width), F32),
        ),
        in_specs=[pl.BlockSpec(memory_space=pltpu.SMEM)] + [vm] * 6,
        out_specs=(vm,) * 9,
        scratch_shapes=[
            pltpu.VMEM((COLS, width), BF),
            pltpu.VMEM((count + 2 * COLS, width), BF),
            dma((6, CHUNKS)), dma((6, CHUNKS)), dma((6,)), dma((6,)), dma(()), dma(()),
        ],
        compiler_params=pltpu.CompilerParams(collective_id=0, has_side_effects=True),
        name="fetch",
    )(level, tokens, cotangent, scale, shared, output, taps)


def reduce_kernel(
    frames, out_ref, base_ref, w_ref, lat_ref, wsum_ref,
    rb, sb, wp, ws, wr, ssem, rsem, ps, pr, rs_s, rs_r, ag_s, ag_r, fw_s, fw_r,
):
    f = lax.axis_index("frame")
    r = lax.axis_index("row")
    tokens = base_ref.shape[0]
    odd = lax.rem(f, 2)
    pair = f + 1 - 2 * odd
    lo2, hi2, lo4, hi4 = f >= 2, f + 2 < frames, f >= 4, f + 4 < frames
    always = f >= 0
    side = ((odd == 1) & (f + 1 < frames)) | ((odd == 0) & (f >= 1))
    relay = ((odd == 1) & lo2) | ((odd == 0) & hi2)
    partner = {"row": 1 - r}
    up, down, across = {"frame": f + 2}, {"frame": f - 2}, {"frame": pair}

    barrier = pltpu.get_barrier_semaphore()
    pl.semaphore_signal(barrier, inc=1, device_id=partner, device_id_type=MESH)

    def hello(k, carry):
        pl.semaphore_signal(
            barrier, inc=1, device_id={"frame": lax.rem(f + k, frames)}, device_id_type=MESH
        )
        return carry

    lax.fori_loop(1, frames, hello, 0)
    pl.semaphore_wait(barrier, frames)

    step = tokens // CHUNKS
    sent = (hi2, lo2, always, hi4, lo4, side)
    got = (lo2, hi2, always, lo2 & hi2, lo2 & hi2, relay)
    device = (up, down, across, up, down, across)

    def copy(kind, c, source):
        part = pl.ds(c * step, step)
        return pltpu.make_async_remote_copy(
            source.at[part], rb.at[kind, part], ssem.at[kind, c], rsem.at[kind, c],
            device_id=device[kind], device_id_type=MESH,
        )

    halves = pltpu.make_async_remote_copy(
        w_ref.at[1 - r], wp, ps, pr, device_id=partner, device_id_type=MESH
    )
    halves.start()
    for c in range(CHUNKS):
        for kind in (3, 4, 5):

            @pl.when(sent[kind])
            def _():
                copy(kind, c, out_ref.at[kind]).start()

    for kind in (0, 1, 3, 4, 5):

        @pl.when(jnp.logical_not(got[kind]))
        def _():
            rb[kind, :, :] = jnp.zeros((tokens, rb.shape[2]), BF)

    halves.wait()
    ws[...] = (w_ref[r] + wp[...]).astype(BF)

    def piece(ref, mine, other, target, s_sem, r_sem, slot, k):
        return pltpu.make_async_remote_copy(
            mine, other, s_sem.at[k], r_sem.at[slot],
            device_id={"frame": target}, device_id_type=MESH,
        )

    def scatter(k):
        target = lax.rem(f + k, frames)
        return piece(ws, ws.at[target], wr.at[f], target, rs_s, rs_r, f, k)

    def arrived(k):
        source = lax.rem(f - k + frames, frames)
        return source, piece(ws, ws.at[source], wr.at[source], source, rs_s, rs_r, source, k)

    def gather(k):
        target = lax.rem(f + k, frames)
        return piece(ws, wsum_ref.at[r, f], wsum_ref.at[r, f], target, ag_s, ag_r, f, k)

    def gathered(k):
        source = lax.rem(f - k + frames, frames)
        return source, piece(
            ws, wsum_ref.at[r, source], wsum_ref.at[r, source], source, ag_s, ag_r, source, k
        )

    def forward(j, own):
        return pltpu.make_async_remote_copy(
            wsum_ref.at[own, j], wsum_ref.at[own, j], fw_s.at[j], fw_r.at[j],
            device_id=partner, device_id_type=MESH,
        )

    def run(body):
        lax.fori_loop(1, frames, lambda k, carry: (body(k), carry)[1], 0)

    run(lambda k: scatter(k).start())
    for c in range(CHUNKS):
        copy(2, c, out_ref.at[2]).start()

    even = jnp.where(odd == 0, 1.0, 0.0).astype(F32)
    for c in range(CHUNKS):
        part = slice(c * step, (c + 1) * step)
        for kind in (3, 4, 5):

            @pl.when(got[kind])
            def _():
                copy(kind, c, out_ref.at[kind]).wait_recv()

        extra = rb[5, part, :].astype(F32)
        rising = out_ref[0, part, :].astype(F32) + rb[3, part, :].astype(F32) + extra * even
        falling = (
            out_ref[1, part, :].astype(F32) + rb[4, part, :].astype(F32) + extra * (1.0 - even)
        )
        sb[0, part, :] = rising.astype(BF)
        sb[1, part, :] = falling.astype(BF)

        @pl.when(hi2)
        def _():
            copy(0, c, sb.at[0]).start()

        @pl.when(lo2)
        def _():
            copy(1, c, sb.at[1]).start()

    def add_piece(k, total):
        source, waiting = arrived(k)
        waiting.wait_recv()
        return total + wr[source].astype(F32)

    total = lax.fori_loop(1, frames, add_piece, w_ref[r, f] + wp[f])
    wsum_ref[r, f] = total.astype(BF)
    run(lambda k: gather(k).start())
    forward(f, r).start()

    for c in range(CHUNKS):
        part = slice(c * step, (c + 1) * step)
        for kind in (0, 1, 2):

            @pl.when(got[kind])
            def _():
                copy(kind, c, out_ref.at[kind]).wait_recv()

        lat_ref[part, :] = (
            base_ref[part, :]
            + rb[0, part, :].astype(F32)
            + rb[1, part, :].astype(F32)
            + rb[2, part, :].astype(F32)
        ).astype(BF)

    def pass_on(k):
        source, waiting = gathered(k)
        waiting.wait_recv()
        forward(source, r).start()

    run(pass_on)

    def finish(k):
        scatter(k).wait_send()
        gather(k).wait_send()

    run(finish)

    def last(j, carry):
        forward(j, r).wait_send()
        forward(j, 1 - r).wait_recv()
        return carry

    lax.fori_loop(0, frames, last, 0)
    for kind in range(6):

        @pl.when(sent[kind])
        def _():
            for c in range(CHUNKS):
                copy(kind, c, out_ref.at[kind]).wait_send()


def reduce(outgoing, base, grads, frames):
    count, width = base.shape
    vm = pl.BlockSpec(memory_space=pltpu.VMEM)
    dma = pltpu.SemaphoreType.DMA
    pieces = grads.shape[1:]
    return pl.pallas_call(
        functools.partial(reduce_kernel, frames),
        out_shape=(
            jax.ShapeDtypeStruct((count, width), BF),
            jax.ShapeDtypeStruct(grads.shape, BF),
        ),
        in_specs=[vm] * 3,
        out_specs=(vm,) * 2,
        scratch_shapes=[
            pltpu.VMEM((6, count, width), BF),
            pltpu.VMEM((2, count, width), BF),
            pltpu.VMEM(pieces, F32),
            pltpu.VMEM(pieces, BF),
            pltpu.VMEM(pieces, BF),
            dma((6, CHUNKS)), dma((6, CHUNKS)), dma(()), dma(()),
            dma((frames,)), dma((frames,)), dma((frames,)), dma((frames,)),
            dma((frames,)), dma((frames,)),
        ],
        compiler_params=pltpu.CompilerParams(collective_id=1, has_side_effects=True),
        name="reduce",
    )(outgoing, base, grads)


def from_partner(value):
    return lax.ppermute(value, "row", [(0, 1), (1, 0)])


def row_halo(array, row_id, width):
    length = array.shape[-3]
    first = lax.slice_in_dim(array, 0, width, axis=array.ndim - 3)
    last = lax.slice_in_dim(array, length - width, length, axis=array.ndim - 3)
    got = from_partner(jnp.where(row_id == 0, last, first))
    zero = jnp.zeros_like(got)
    before = jnp.where(row_id == 0, zero, got)
    after = jnp.where(row_id == 0, got, zero)
    return jnp.concatenate([before, array, after], axis=array.ndim - 3)


def local(
    latents, ref_frames, windows, quant_level, quant_scale,
    shared_proj, value_proj, output_proj, conv_taps, cotangent,
):
    width = latents.shape[2]
    rows_dev = latents.shape[1] // COLS
    row_devs = lax.axis_size("row")
    total_rows = rows_dev * row_devs
    frame_id = lax.axis_index("frame")
    row_id = lax.axis_index("row")
    own_refs = ref_frames[0]
    ext_rows = rows_dev + 2 * WMAX
    grid = (rows_dev, COLS, width)
    tokens = latents[0]
    frames = lax.axis_size("frame")
    odd = frame_id % 2
    sources = (
        frame_id - 2, frame_id + 2, frame_id + 1 - 2 * odd,
        frame_id - 4, frame_id + 4, frame_id - 1 + 2 * odd,
    )
    buf, halo, q, qt, do, dot, grad_zb, grad_resid, gain = fetch(
        quant_level, tokens, cotangent[0], quant_scale, shared_proj, output_proj, conv_taps, frames
    )
    kinds = jnp.zeros((2,), jnp.int32)
    for kind, source in enumerate(sources):
        kinds = jnp.where(own_refs == source, kind, kinds)
    rest = jnp.stack([windows[0], row_id, jnp.int32(total_rows)]).astype(jnp.int32)
    meta = jnp.concatenate([kinds, rest])
    residual, hidden, grad_latents, partial, grad_shared, grad_values, grad_output = attention(
        meta, buf, halo, tokens, q, qt, do, dot, grad_resid, shared_proj, value_proj, output_proj
    )
    hidden_ext = row_halo(hidden.reshape(grid), row_id, 1).reshape(-1, width)
    context = residual
    for t in range(3):
        context = context + mm(hidden_ext[t * COLS : (t + rows_dev) * COLS], conv_taps[t])
    coded = (context * gain).astype(BF)

    partial = partial.reshape(2, ext_rows, COLS, width)
    upper = partial[:, :WMAX]
    lower = partial[:, WMAX + rows_dev :]
    got = from_partner(jnp.where(row_id == 0, lower, upper).astype(BF)).astype(F32)
    filler = jnp.zeros((2, rows_dev - WMAX, COLS, width), F32)
    middle = (
        partial[:, WMAX : WMAX + rows_dev]
        + jnp.concatenate([jnp.where(row_id == 0, 0.0, got), filler], axis=1)
        + jnp.concatenate([filler, jnp.where(row_id == 0, got, 0.0)], axis=1)
    )
    targets = (
        frame_id + 2, frame_id - 2, frame_id + 1 - 2 * odd,
        frame_id + 4, frame_id - 4, frame_id - 1 + 2 * odd,
    )
    outgoing = jnp.stack(
        [
            jnp.sum(jnp.where((own_refs == t).reshape(2, 1, 1, 1), middle, 0.0), axis=0)
            .astype(BF)
            .reshape(-1, width)
            for t in targets
        ]
    )
    grad_taps = jnp.stack(
        [mm(hidden_ext[t * COLS : (t + rows_dev) * COLS], grad_zb, 0, 0) for t in range(3)]
    )
    stacked = jnp.concatenate(
        [grad_shared, grad_values, grad_output, grad_taps.reshape(-1, width)], axis=0
    )
    grads = stacked.reshape(2, frames, stacked.shape[0] // (2 * frames), width)
    new_latents, summed = reduce(outgoing, grad_latents, grads, frames)
    norm = 1.0 / math.sqrt(frames * total_rows * COLS)
    summed = summed.reshape(-1, width).astype(F32) * norm
    return (
        coded[None],
        new_latents[None],
        summed[:width],
        summed[width : 2 * width],
        summed[2 * width : 3 * width],
        summed[3 * width :].reshape(3, width, width),
    )


def solution(mesh):
    tok = P(("groups", "frame"), "row", None)
    frm = P(("groups", "frame"))
    placed = (tok, P(("groups", "frame"), None), frm, frm, P(), P(), P(), P(), P(), tok)
    return jax.shard_map(
        local,
        mesh=mesh,
        in_specs=placed,
        out_specs=(
            tok, tok, P("groups", None), P("groups", None), P("groups", None),
            P("groups", None, None),
        ),
        check_vma=False,
    )
```

profile of v0, /device:TPU:0, one launch (start us, length us, event | category | flops | bytes accessed | tf_op | source)
XLA Modules:
  0.0 102.9 jit_solution(12024245787312903546)
XLA Ops:
  1.9 0.7 select_select_fusion
  2.6 0.6 pad_add_fusion.meta_ref
  3.2 20.9 %fetch.1 = (bf16[6,512,256]{2,1,0:T(8,128)(2,1)}, bf16[6,128,256]{2,1,0:T(8,128)(2,1)}, bf16[512,256]{1,0:T(8,128)(2,1)}, bf16[256,512]{1,0:T(8,128)(2,1)}, bf16...) custom-call(s32[1]{0:T(128)S(6)} %copy.23.level_ref, ...), custom_call_target="tpu_custom_call" | custom-call | tf_op jit(solution)/shard_map/fetch/pallas_call | solution.py:393
  24.1 0.0 copy-start.11
  24.1 0.0 copy-start.1
  24.1 28.5 %attention.1 = (f32[512,256]{1,0:T(8,128)}, bf16[512,256]{1,0:T(8,128)(2,1)}, f32[512,256]{1,0:T(8,128)}, f32[2,768,256]{2,1,0:T(8,128)}, f32[256,256]{1,0:T(8,1...) custom-call(s32[5]{0:T(128)} %pad_add_fusion.meta_ref, bf16[6,512,256]{2,1,0:T(8,128)(2,1)} %get-tuple-element.24.buf_hbm, ...), custom_call_target="tpu_custom_call" | custom-call | flops 20000000000 | bytes 8000000 | tf_op jit(solution)/shard_map/attention/pallas_call | solution.py:189
  52.6 0.0 copy-start
  52.7 0.0 copy-start.3
  52.7 0.0 copy-start.5
  52.7 0.9 select_bitcast_fusion
  53.6 0.3 collective-permute-start
  53.9 1.1 %fusion.4 = bf16[2,2,64,256]{3,2,1,0:T(8,128)(2,1)S(1)} fusion(f32[2,12,64,256]{3,2,1,0:T(8,128)} %bitcast.84, pred[]{:T(512)S(6)} %eq.115), kind=kLoop, calls=%fused_computation.23 | loop fusion | flops 65536 | bytes 393217 | tf_op jit(solution)/shard_map/convert_element_type | solution.py:671
  55.0 0.2 collective-permute-start.1
  55.2 0.0 copy-done.11
  55.2 0.0 copy-done.1
  55.2 1.2 %convolution_bitcast_fusion.1 = f32[1,256,256]{2,1,0:T(8,128)S(1)} fusion(bf16[512,256]{1,0:T(8,128)(2,1)} %get-tuple-element.32, bf16[512,256]{1,0:T(8,128)(2,1)S(1)} %copy-done.1), kind=kOutput, calls=%fused_computation.8 | convolution fusion | flops 67108864 | bytes 786432 | tf_op jit(solution)/shard_map/dot_general | solution.py:24
  56.4 0.0 collective-permute-done
  56.5 0.0 copy-done
  56.5 0.3 convolution_bitcast_fusion.2
  56.8 0.0 copy-done.3
  56.8 0.0 copy-done.5
  56.8 0.2 convolution_add_fusion.2
  57.0 0.0 copy-start.6
  57.1 0.0 copy-start.7
  57.1 0.0 copy-start.8
  57.1 0.2 convolution_add_fusion.1
  57.3 0.3 convolution_bitcast_fusion
  57.6 0.1 pad_maximum_fusion.1
  57.6 0.3 copy-done.6
  58.0 0.1 copy-done.7
  58.1 0.1 copy-done.8
  58.2 0.0 copy-start.10
  58.2 1.2 %pad_maximum_fusion = f32[1536,256]{1,0:T(8,128)} fusion(f32[768,256]{1,0:T(8,128)S(1)} %bitcast.78, f32[256,256]{1,0:T(8,128)S(1)} %copy-done.8, f32[256,256]{1,0:T(8,128)S(1)} %copy-done.7, f32[256,256]{1,0:T(8,128)S(1)} %copy-done.6), kind=kLoop, calls=%fused_computation | loop fusion | flops 1179648 | bytes 3145728 | tf_op jit(solution)/shard_map/concatenate | solution.py:693
  59.4 0.0 copy-done.10
  59.4 0.9 fusion.2
  60.4 0.0 collective-permute-done.1
  60.4 0.9 convert_select_fusion.1
  61.3 0.0 copy-done.4
  61.3 0.5 select_reduce_fusion
  62.0 0.0 copy-start.2
  62.0 1.1 %copy-done.2 = bf16[6,512,256]{2,1,0:T(8,128)(2,1)} copy-done((bf16[6,512,256]{2,1,0:T(8,128)(2,1)}, bf16[6,512,256]{2,1,0:T(8,128)(2,1)S(1)}, u32[]{:S(2)}) %copy-start.2) | copy-done | bytes 1572888
  63.2 35.8 %reduce.1 = (bf16[512,256]{1,0:T(8,128)(2,1)}, bf16[2,8,96,256]{3,2,1,0:T(8,128)(2,1)}) custom-call(bf16[6,512,256]{2,1,0:T(8,128)(2,1)} %copy-done.2, f32[512,256]{1,0:T(8,128)} %get-tuple-element.35.base_ref, f32[2,8,96,256]{3,2,1,0:T(8,128)} %bitcast.76), custom_call_target="tpu_custom_call" | custom-call | tf_op jit(solution)/shard_map/reduce/pallas_call | solution.py:593
  99.1 1.3 %convert_multiply_fusion = f32[2,8,96,256]{3,2,1,0:T(8,128)S(1)} fusion(bf16[2,8,96,256]{3,2,1,0:T(8,128)(2,1)} %get-tuple-element.41), kind=kLoop, calls=%fused_computation.1 | loop fusion | flops 786432 | bytes 2359296 | tf_op jit(solution)/shard_map/mul | solution.py:699
  100.4 0.0 copy-start.9
  100.4 0.9 slice.80
  101.3 0.9 fusion.11
  102.2 0.0 copy-done.9
  102.2 0.7 copy.24
  (10 shorter events, 0.2 us)
Async XLA Ops:
  24.1 31.1 %copy-start.11 = (s32[1,2]{1,0:T(1,128)S(1)}, s32[1,2]{1,0:T(1,128)}, u32[]{:S(2)}) copy-start(s32[1,2]{1,0:T(1,128)} %param.11) | copy-start | bytes 28
  24.1 31.1 %copy-start.1 = (bf16[512,256]{1,0:T(8,128)(2,1)S(1)}, bf16[512,256]{1,0:T(8,128)(2,1)}, u32[]{:S(2)}) copy-start(bf16[512,256]{1,0:T(8,128)(2,1)} %get-tuple-element.39) | copy-start | bytes 786436
  52.6 3.8 %copy-start = (bf16[512,256]{1,0:T(8,128)(2,1)S(1)}, bf16[512,256]{1,0:T(8,128)(2,1)}, u32[]{:S(2)}) copy-start(bf16[512,256]{1,0:T(8,128)(2,1)} %get-tuple-element.32) | copy-start | bytes 786436
  52.7 4.1 %copy-start.3 = (bf16[3,256,256]{2,1,0:T(8,128)(2,1)S(1)}, bf16[3,256,256]{2,1,0:T(8,128)(2,1)}, u32[]{:S(2)}) copy-start(bf16[3,256,256]{2,1,0:T(8,128)(2,1)} %taps_ref.1) | copy-start | bytes 1179652
  52.7 4.1 %copy-start.5 = (f32[512,256]{1,0:T(8,128)S(1)}, f32[512,256]{1,0:T(8,128)}, u32[]{:S(2)}) copy-start(f32[512,256]{1,0:T(8,128)} %get-tuple-element.31) | copy-start | bytes 1572868
  53.6 2.9 %collective-permute-start = (bf16[1,64,256]{2,1,0:T(8,128)(2,1)S(1)}, bf16[1,64,256]{2,1,0:T(8,128)(2,1)S(1)}, u32[]{:S(2)}, u32[]{:S(2)}) collective-permute-start(bf16[1,64,256]{2,1,0:T(8,128)(2,1)S(1)} %select_bitcast_fusion), channel_id=1, source_target_pairs={{0,1},{1,0},{2,3},{3,2},{4,5},{5,4},{6,7},{7,6},{8,9},{9,8},{10,11... | collective-permute-start | bytes 98312 | tf_op jit(solution)/shard_map/ppermute | solution.py:617
  55.0 5.4 %collective-permute-start.1 = (bf16[2,2,64,256]{3,2,1,0:T(8,128)(2,1)S(1)}, bf16[2,2,64,256]{3,2,1,0:T(8,128)(2,1)}, u32[]{:S(2)}, u32[]{:S(2)}) collective-permute-start(bf16[2,2,64,256]{3,2,1,0:T(8,128)(2,1)S(1)} %fusion.4), channel_id=1, source_target_pairs={{0,1},{1,0},{2,3},{3,2},{4,5},{5,4},{6,7},{7,6},{8,9},{9,8},{10,11... | collective-permute-start | bytes 393224 | tf_op jit(solution)/shard_map/ppermute | solution.py:617
  57.0 1.0 copy-start.6
  57.1 1.0 copy-start.7
  57.1 1.1 %copy-start.8 = (f32[256,256]{1,0:T(8,128)S(1)}, f32[256,256]{1,0:T(8,128)}, u32[]{:S(2)}) copy-start(f32[256,256]{1,0:T(8,128)} %get-tuple-element.38) | copy-start | bytes 786436
  58.2 1.3 %copy-start.10 = (f32[1,256]{1,0:T(1,128)S(1)}, f32[1,256]{1,0:T(1,128)}, u32[]{:S(2)}) copy-start(f32[1,256]{1,0:T(1,128)} %get-tuple-element.33) | copy-start | bytes 3076
  59.4 1.9 %copy-start.4 = (f32[2,768,256]{2,1,0:T(8,128)S(1)}, f32[2,768,256]{2,1,0:T(8,128)}, u32[]{:S(2)}) copy-start(f32[2,768,256]{2,1,0:T(8,128)} %get-tuple-element.34) | copy-start | bytes 4718596
  62.0 1.2 %copy-start.2 = (bf16[6,512,256]{2,1,0:T(8,128)(2,1)}, bf16[6,512,256]{2,1,0:T(8,128)(2,1)S(1)}, u32[]{:S(2)}) copy-start(bf16[6,512,256]{2,1,0:T(8,128)(2,1)S(1)} %bitcast_dynamic-update-slice_fusion.out_ref) | copy-start | bytes 4718596
  100.4 1.8 %copy-start.9 = (bf16[512,256]{1,0:T(8,128)(2,1)S(1)}, bf16[512,256]{1,0:T(8,128)(2,1)}, u32[]{:S(2)}) copy-start(bf16[512,256]{1,0:T(8,128)(2,1)} %get-tuple-element.40) | copy-start | bytes 786436
where the time goes:
time: 103 us
  Pallas kernels  85.2 us (83%)
  other arithmetic  7.33 us (7%)
  local copies, waits for them, and re-layouts  4.36 us (4%)
  matrix products  3.15 us (3%)
  between operations  2.24 us (2%)
    pallas_call x1, Pallas kernels, reduce(): pl.pallas_call(functools.partial(reduce_kernel, frames), out_shape=(jax.S...  35.8 us
    pallas_call x1, Pallas kernels, attention(): pl.pallas_call(attention_kernel, out_shape=(full, jax.ShapeDtypeStruct((t...  28.5 us
    pallas_call x1, Pallas kernels, fetch(): pl.pallas_call(functools.partial(fetch_kernel, frames), out_shape=(jax.Sh...  20.9 us
    dot_general x6, matrix products, mm(): lax.dot_general(a, b, (((ca,), (cb,)), ((), ())), preferred_element_type=...  3.15 us
    unnamed x30, local copies, waits for them, and re-layouts  2.51 us
  transfers between devices with their start and end apart: 2, of which 0 were waited for; matrix products, arithmetic and copies ran while one was open for 5% of the time, Pallas kernels for 0%

commit v1 on v0

--- a/solution.py
+++ b/solution.py
@@ -11,7 +11,6 @@
 HEADS = 8
 DH = 32
 COLS = 64
-QBLK = 4
 WMAX = 2
 
 SCORE_SCALE = 1.5 / math.sqrt(DH)
@@ -24,165 +23,213 @@
     return lax.dot_general(a, b, (((ca,), (cb,)), ((), ())), preferred_element_type=F32)
 
 
+HALF = 4
+
+
+def masked_rows(block, f0):
+    lane = lax.broadcasted_iota(jnp.int32, (1, HALF * DH), 1) // DH
+    part = block[:, f0 : f0 + HALF * DH]
+    return jnp.concatenate(
+        [jnp.where(lane == h, part, jnp.zeros_like(part)) for h in range(HALF)], axis=0
+    )
+
+
+def head_diagonal(wide):
+    rows = wide.T
+    lane = lax.broadcasted_iota(jnp.int32, (1, HALF * DH), 1) // DH
+    out = rows[:COLS]
+    for h in range(1, HALF):
+        out = jnp.where(lane == h, rows[h * COLS : (h + 1) * COLS], out)
+    return out
+
+
+def forward_row(i, bias, k_ref, qm_ref, p_ref, pb_ref, inv_ref):
+    band = 2 * COLS
+    reach = 2 * WMAX + 1
+    wide = HALF * COLS
+    base = i * band
+    kk = SCORE_SCALE * LOG2E
+    for hf in range(2):
+        f0 = hf * HALF * DH
+        ft = slice(f0, f0 + HALF * DH)
+        p_ref[i, hf] = mm(k_ref[base : base + reach * band, ft], qm_ref[i, hf], 1, 1)
+        m8 = None
+        for c in range(reach):
+            x = p_ref[i, hf, c * band : (c + 1) * band, :].reshape(band // 8, 8, wide)
+            top = jnp.max(x, axis=0) + bias[c]
+            m8 = top if m8 is None else jnp.maximum(m8, top)
+        m = jnp.max(m8, axis=0, keepdims=True)
+        l8 = jnp.zeros((8, wide), F32)
+        for c in range(reach):
+            sl = slice(c * band, (c + 1) * band)
+            p = jnp.exp2(p_ref[i, hf, sl, :] * kk + (bias[c] - m) * kk)
+            p_ref[i, hf, sl, :] = p
+            l8 = l8 + jnp.sum(p.reshape(band // 8, 8, wide), axis=0)
+        inv = 1.0 / jnp.sum(l8, axis=0, keepdims=True)
+        inv_ref[i, hf] = inv
+        for c in range(reach):
+            sl = slice(c * band, (c + 1) * band)
+            pb_ref[i, hf, sl, :] = (p_ref[i, hf, sl, :] * inv).astype(BF)
+
+
+def mix_row(i, vt_ref, pb_ref, mix_ref):
+    band = 2 * COLS
+    reach = 2 * WMAX + 1
+    base = i * band
+    for hf in range(2):
+        f0 = hf * HALF * DH
+        ft = slice(f0, f0 + HALF * DH)
+        mix = mm(vt_ref[ft, base : base + reach * band], pb_ref[i, hf])
+        mix_ref[i * COLS : (i + 1) * COLS, ft] = head_diagonal(mix).astype(BF)
+
+
+def score_row(i, v_ref, dom_ref, p_ref, inv_ref, dp_ref, ds_ref):
+    band = 2 * COLS
+    reach = 2 * WMAX + 1
+    wide = HALF * COLS
+    base = i * band
+    win = slice(base, base + reach * band)
+    for hf in range(2):
+        f0 = hf * HALF * DH
+        ft = slice(f0, f0 + HALF * DH)
+        dp_ref[i, hf] = mm(v_ref[win, ft], dom_ref[i, hf], 1, 1)
+        u8 = jnp.zeros((8, wide), F32)
+        for c in range(reach):
+            sl = slice(c * band, (c + 1) * band)
+            x = p_ref[i, hf, sl, :] * dp_ref[i, hf, sl, :]
+            u8 = u8 + jnp.sum(x.reshape(band // 8, 8, wide), axis=0)
+        inv = inv_ref[i, hf]
+        ci = inv * SCORE_SCALE
+        inner = jnp.sum(u8, axis=0, keepdims=True) * inv * ci
+        for c in range(reach):
+            sl = slice(c * band, (c + 1) * band)
+            ds_ref[i, hf, sl, :] = (p_ref[i, hf, sl, :] * (dp_ref[i, hf, sl, :] * ci - inner)).astype(BF)
+
+
+def query_row(i, kt_ref, ds_ref, dq_ref):
+    band = 2 * COLS
+    base = i * band
+    win = slice(base, base + (2 * WMAX + 1) * band)
+    for hf in range(2):
+        f0 = hf * HALF * DH
+        ft = slice(f0, f0 + HALF * DH)
+        dq = mm(kt_ref[ft, win], ds_ref[i, hf])
+        dq_ref[i * COLS : (i + 1) * COLS, ft] = head_diagonal(dq).astype(BF)
+
+
+def key_row(i, qm_ref, dom_ref, pb_ref, ds_ref, dk_ref, dv_ref):
+    band = 2 * COLS
+    base = i * band
+    win = slice(base, base + (2 * WMAX + 1) * band)
+    for hf in range(2):
+        f0 = hf * HALF * DH
+        ft = slice(f0, f0 + HALF * DH)
+        dk_ref[win, ft] += mm(ds_ref[i, hf], qm_ref[i, hf])
+        dv_ref[win, ft] += mm(pb_ref[i, hf], dom_ref[i, hf])
+
+
 def attention_kernel(
-    meta_ref, buf_hbm, halo_hbm, x_hbm, q_hbm, qt_hbm, do_hbm, dot_hbm, resid_hbm,
+    meta_ref, buf_hbm, halo_hbm, x_hbm, q_hbm, do_hbm, resid_hbm,
     sp_ref, vp_ref, op_ref,
     residual_ref, hidden_ref, base_ref, part_ref, gs_ref, gv_ref, go_ref,
-    xs_ref, k_ref, v_ref, kt_ref, vt_ref, mixt_ref, dqt_ref, dk_ref, dv_ref,
-    s_scr, dp_scr, p_scr, ds_scr, qm_scr, dom_scr,
-    x_ref, q_ref, qt_ref, do_ref, dot_ref, resid_ref, sems,
+    xs_ref, xi_ref, k_ref, v_ref, kt_ref, vt_ref, mix_ref, dq_ref, dk_ref, dv_ref,
+    p_ref, pb_ref, inv_ref, dp_ref, ds_ref, qm_ref, dom_ref,
+    x_ref, q_ref, do_ref, resid_ref, sems,
 ):
     tokens, width = q_ref.shape
-    nq = QBLK * COLS
-    span = (QBLK + 2 * WMAX) * COLS
-    rows = span // COLS
-    blocks = tokens // nq
-    half = width // 2
-    per_half = HEADS // 2
-    lane = lax.broadcasted_iota(jnp.int32, (1, width), 1) // DH
-    sub = lax.broadcasted_iota(jnp.int32, (half, 1), 0) // DH
-
-    dk_ref[...] = jnp.zeros_like(dk_ref)
-    dv_ref[...] = jnp.zeros_like(dv_ref)
+    rows = tokens // COLS
     rim = WMAX * COLS
     window = meta_ref[2]
     row_id = meta_ref[3]
-    first_row = row_id * (tokens // COLS)
+    first_row = row_id * rows
     total_rows = meta_ref[4]
     bottom = rim + tokens
     held = pl.multiple_of(jnp.where(row_id == 0, bottom, 0), rim)
     empty = pl.multiple_of(jnp.where(row_id == 0, 0, bottom), rim)
-    moves = []
+    moves = [(q_hbm, q_ref), (do_hbm, do_ref)]
     for s in range(2):
         kind = meta_ref[s]
         moves.append((buf_hbm.at[kind], xs_ref.at[s, pl.ds(rim, tokens)]))
         moves.append((halo_hbm.at[kind], xs_ref.at[s, pl.ds(held, rim)]))
-    moves += [
-        (q_hbm, q_ref), (do_hbm, do_ref), (qt_hbm, qt_ref), (dot_hbm, dot_ref),
-        (x_hbm, x_ref), (resid_hbm, resid_ref),
-    ]
+    moves += [(x_hbm, x_ref), (resid_hbm, resid_ref)]
     copies = [
         pltpu.make_async_copy(source, target, sems.at[i])
         for i, (source, target) in enumerate(moves)
     ]
     for move in copies:
         move.start()
+    dk_ref[...] = jnp.zeros_like(dk_ref)
+    dv_ref[...] = jnp.zeros_like(dv_ref)
+    copies[0].wait()
+    copies[1].wait()
+    for i in range(rows):
+        tok = slice(i * COLS, (i + 1) * COLS)
+        for hf in range(2):
+            qm_ref[i, hf] = masked_rows(q_ref[tok, :], hf * HALF * DH)
+            dom_ref[i, hf] = masked_rows(do_ref[tok, :], hf * HALF * DH)
     for s in range(2):
         xs_ref[s, pl.ds(empty, rim), :] = jnp.zeros((rim, width), BF)
-        copies[2 * s].wait()
-        copies[2 * s + 1].wait()
-        xs = xs_ref[s]
-        keys = mm(xs, sp_ref[...]).astype(BF)
-        vals = mm(xs, vp_ref[...]).astype(BF)
-        k_ref[s] = keys
-        v_ref[s] = vals
-        kt_ref[s] = keys.T
-        vt_ref[s] = vals.T
-    for move in copies[4:]:
+        copies[2 * s + 2].wait()
+        copies[2 * s + 3].wait()
+        for e in range(rows + 2 * WMAX):
+            xi_ref[(2 * e + s) * COLS : (2 * e + s + 1) * COLS, :] = xs_ref[
+                s, e * COLS : (e + 1) * COLS, :
+            ]
+    xi = xi_ref[...]
+    keys = mm(xi, sp_ref[...]).astype(BF)
+    k_ref[...] = keys
+    kt_ref[...] = keys.T
+    vals = mm(xi, vp_ref[...]).astype(BF)
+    v_ref[...] = vals
+    vt_ref[...] = vals.T
+
+    def bias_of(i):
+        out = []
+        for c in range(2 * WMAX + 1):
+            key_row = first_row + i + c - WMAX
+            inside = (key_row >= 0) & (key_row < total_rows) & (abs(c - WMAX) <= window)
+            out.append(jnp.where(inside, 0.0, -jnp.inf).astype(F32))
+        return out
+
+    for i in range(rows):
+        forward_row(i, bias_of(i), k_ref, qm_ref, p_ref, pb_ref, inv_ref)
+    for i in range(rows):
+        mix_row(i, vt_ref, pb_ref, mix_ref)
+    for i in range(rows + 1):
+        if i < rows:
+            score_row(i, v_ref, dom_ref, p_ref, inv_ref, dp_ref, ds_ref)
+        if i:
+            key_row(i - 1, qm_ref, dom_ref, pb_ref, ds_ref, dk_ref, dv_ref)
+            query_row(i - 1, kt_ref, ds_ref, dq_ref)
+    for move in copies[6:]:
         move.wait()
-    query_row = lax.broadcasted_iota(jnp.int32, (1, nq), 1) // COLS
-
-    def bias_row(b, c):
-        key_row = first_row + b * QBLK + c - WMAX
-        reach = jnp.where((key_row >= 0) & (key_row < total_rows), window, -1)
-        return jnp.where(jnp.abs(c - WMAX - query_row) <= reach, 0.0, -jnp.inf).astype(F32)
-
-    for b in range(blocks):
-        q0 = b * nq
-        qb = q_ref[q0 : q0 + nq, :]
-        dob = do_ref[q0 : q0 + nq, :]
-        for h in range(HEADS):
-            keep = lane == h
-            qm_scr[h * nq : (h + 1) * nq, :] = jnp.where(keep, qb, jnp.zeros_like(qb))
-            dom_scr[h * nq : (h + 1) * nq, :] = jnp.where(keep, dob, jnp.zeros_like(dob))
-
-        for hf in range(2):
-            f0 = hf * half
-            qth = qt_ref[f0 : f0 + half, q0 : q0 + nq]
-            doth = dot_ref[f0 : f0 + half, q0 : q0 + nq]
-
-            def one_head(hh, carry, hf=hf, f0=f0, qth=qth, doth=doth, q0=q0, b=b):
-                keep = sub == hh
-                qtm = jnp.where(keep, qth, jnp.zeros_like(qth))
-                dotm = jnp.where(keep, doth, jnp.zeros_like(doth))
-                for s in range(2):
-                    s_scr[s * span : (s + 1) * span, :] = mm(
-                        k_ref[s, q0 : q0 + span, f0 : f0 + half], qtm
-                    )
-                    dp_scr[s * span : (s + 1) * span, :] = mm(
-                        v_ref[s, q0 : q0 + span, f0 : f0 + half], dotm
-                    )
-                m8 = jnp.full((8, nq), -jnp.inf, F32)
-                for c in range(2 * rows):
-                    x = s_scr[c * COLS : (c + 1) * COLS, :].reshape(COLS // 8, 8, nq)
-                    m8 = jnp.maximum(m8, jnp.max(x, axis=0) + bias_row(b, c % rows))
-                m = jnp.max(m8, axis=0, keepdims=True)
-                kk = SCORE_SCALE * LOG2E
-                l8 = jnp.zeros((8, nq), F32)
-                u8 = jnp.zeros((8, nq), F32)
-                for c in range(2 * rows):
-                    sl = slice(c * COLS, (c + 1) * COLS)
-                    off = (bias_row(b, c % rows) - m) * kk
-                    p = jnp.exp2(s_scr[sl, :] * kk + off)
-                    s_scr[sl, :] = p
-                    l8 = l8 + jnp.sum(p.reshape(COLS // 8, 8, nq), axis=0)
-                    u8 = u8 + jnp.sum((p * dp_scr[sl, :]).reshape(COLS // 8, 8, nq), axis=0)
-                inv = 1.0 / jnp.sum(l8, axis=0, keepdims=True)
-                ci = inv * SCORE_SCALE
-                inner = jnp.sum(u8, axis=0, keepdims=True) * inv * ci
-                col = pl.multiple_of((hf * per_half + hh) * nq, nq)
-                for c in range(2 * rows):
-                    sl = slice(c * COLS, (c + 1) * COLS)
-                    p = s_scr[sl, :]
-                    p_scr[sl, pl.ds(col, nq)] = (p * inv).astype(BF)
-                    ds_scr[sl, pl.ds(col, nq)] = (p * (dp_scr[sl, :] * ci - inner)).astype(BF)
-                r0 = pl.multiple_of(f0 + hh * DH, DH)
-                mix = jnp.zeros((DH, nq), F32)
-                dq = jnp.zeros((DH, nq), F32)
-                for s in range(2):
-                    ks = slice(s * span, (s + 1) * span)
-                    mix = mix + mm(
-                        vt_ref[s, pl.ds(r0, DH), q0 : q0 + span], p_scr[ks, pl.ds(col, nq)]
-                    )
-                    dq = dq + mm(
-                        kt_ref[s, pl.ds(r0, DH), q0 : q0 + span], ds_scr[ks, pl.ds(col, nq)]
-                    )
-                mixt_ref[pl.ds(r0, DH), q0 : q0 + nq] = mix.astype(BF)
-                dqt_ref[pl.ds(r0, DH), q0 : q0 + nq] = dq
-                return carry
-
-            lax.fori_loop(0, per_half, one_head, 0)
-
-        for s in range(2):
-            ks = slice(s * span, (s + 1) * span)
-            dk_ref[s, q0 : q0 + span, :] += mm(ds_scr[ks, :], qm_scr[...])
-            dv_ref[s, q0 : q0 + span, :] += mm(p_scr[ks, :], dom_scr[...])
-
-    dq = dqt_ref[...].T.astype(BF)
+
+    dq = dq_ref[...]
     base_ref[...] = resid_ref[...] + mm(dq, sp_ref[...], 1, 1)
-    mixt = mixt_ref[...]
-    go_ref[...] = mm(mixt, resid_ref[...].astype(BF))
-    residual = x_ref[...].astype(F32) + mm(mixt.T, op_ref[...])
+    mix = mix_ref[...]
+    go_ref[...] = mm(mix.T, resid_ref[...].astype(BF))
+    residual = x_ref[...].astype(F32) + mm(mix, op_ref[...])
     residual_ref[...] = residual
     hidden_ref[...] = residual.astype(BF)
-    gs = mm(x_ref[...].T, dq)
-    gv = jnp.zeros((width, width), F32)
-    for s in range(2):
-        dk = dk_ref[s].astype(BF)
-        dv = dv_ref[s].astype(BF)
-        part_ref[s] = mm(dk, sp_ref[...], 1, 1) + mm(dv, vp_ref[...], 1, 1)
-        xst = xs_ref[s].T
-        gs = gs + mm(xst, dk)
-        gv = gv + mm(xst, dv)
-    gs_ref[...] = gs
-    gv_ref[...] = gv
-
-
-def attention(meta, buf, halo, x, q, qt, do, dot, resid, shared, value, output):
+    dk = dk_ref[...].astype(BF)
+    dv = dv_ref[...].astype(BF)
+    part = mm(dk, sp_ref[...], 1, 1) + mm(dv, vp_ref[...], 1, 1)
+    for e in range(rows + 2 * WMAX):
+        for s in range(2):
+            part_ref[s, e * COLS : (e + 1) * COLS, :] = part[
+                (2 * e + s) * COLS : (2 * e + s + 1) * COLS, :
+            ]
+    xit = xi_ref[...].T
+    gs_ref[...] = mm(x_ref[...].T, dq) + mm(xit, dk)
+    gv_ref[...] = mm(xit, dv)
+
+
+def attention(meta, buf, halo, x, q, do, resid, shared, value, output):
     tokens, width = q.shape
+    rows = tokens // COLS
     ext = tokens + 2 * WMAX * COLS
-    nq = QBLK * COLS
-    keys = 2 * (QBLK + 2 * WMAX) * COLS
+    keys = 2 * (2 * WMAX + 1) * COLS
+    wide = HALF * COLS
     vm = pl.BlockSpec(memory_space=pltpu.VMEM)
     full = jax.ShapeDtypeStruct((tokens, width), F32)
     square = jax.ShapeDtypeStruct((width, width), F32)
@@ -196,39 +243,39 @@
             square, square, square,
         ),
         in_specs=[pl.BlockSpec(memory_space=pltpu.SMEM)]
-        + [pl.BlockSpec(memory_space=pltpu.MemorySpace.HBM)] * 8
+        + [pl.BlockSpec(memory_space=pltpu.MemorySpace.HBM)] * 6
         + [vm] * 3,
         out_specs=(vm,) * 7,
         scratch_shapes=[
             pltpu.VMEM((2, ext, width), BF),
-            pltpu.VMEM((2, ext, width), BF),
-            pltpu.VMEM((2, ext, width), BF),
-            pltpu.VMEM((2, width, ext), BF),
-            pltpu.VMEM((2, width, ext), BF),
-            pltpu.VMEM((width, tokens), BF),
-            pltpu.VMEM((width, tokens), F32),
-            pltpu.VMEM((2, ext, width), F32),
-            pltpu.VMEM((2, ext, width), F32),
-            pltpu.VMEM((keys, nq), F32),
-            pltpu.VMEM((keys, nq), F32),
-            pltpu.VMEM((keys, HEADS * nq), BF),
-            pltpu.VMEM((keys, HEADS * nq), BF),
-            pltpu.VMEM((HEADS * nq, width), BF),
-            pltpu.VMEM((HEADS * nq, width), BF),
+            pltpu.VMEM((2 * ext, width), BF),
+            pltpu.VMEM((2 * ext, width), BF),
+            pltpu.VMEM((2 * ext, width), BF),
+            pltpu.VMEM((width, 2 * ext), BF),
+            pltpu.VMEM((width, 2 * ext), BF),
             pltpu.VMEM((tokens, width), BF),
             pltpu.VMEM((tokens, width), BF),
-            pltpu.VMEM((width, tokens), BF),
+            pltpu.VMEM((2 * ext, width), F32),
+            pltpu.VMEM((2 * ext, width), F32),
+            pltpu.VMEM((rows, 2, keys, wide), F32),
+            pltpu.VMEM((rows, 2, keys, wide), BF),
+            pltpu.VMEM((rows, 2, 1, wide), F32),
+            pltpu.VMEM((rows, 2, keys, wide), F32),
+            pltpu.VMEM((rows, 2, keys, wide), BF),
+            pltpu.VMEM((rows, 2, wide, HALF * DH), BF),
+            pltpu.VMEM((rows, 2, wide, HALF * DH), BF),
             pltpu.VMEM((tokens, width), BF),
-            pltpu.VMEM((width, tokens), BF),
+            pltpu.VMEM((tokens, width), BF),
+            pltpu.VMEM((tokens, width), BF),
             pltpu.VMEM((tokens, width), F32),
-            pltpu.SemaphoreType.DMA((10,)),
+            pltpu.SemaphoreType.DMA((8,)),
         ],
-        compiler_params=pltpu.CompilerParams(vmem_limit_bytes=66_000_000),
+        compiler_params=pltpu.CompilerParams(vmem_limit_bytes=64_000_000),
         cost_estimate=pl.CostEstimate(
             flops=int(2e10), bytes_accessed=int(8e6), transcendentals=int(4e6)
         ),
         name="attention",
-    )(meta, buf, halo, x, q, qt, do, dot, resid, shared, value, output)
+    )(meta, buf, halo, x, q, do, resid, shared, value, output)
 
 
 MESH = pl.DeviceIdType.MESH
@@ -250,7 +297,7 @@
 
 def fetch_kernel(
     frames, level_ref, x_ref, ct_ref, qs_ref, sp_ref, op_ref, taps_ref,
-    buf_ref, halo_ref, q_ref, qt_ref, do_ref, dot_ref, gzb_ref, resid_ref, gain_ref,
+    buf_ref, halo_ref, q_ref, do_ref, gzb_ref, resid_ref, gain_ref,
     cth_ref, ext_ref, ssem, rsem, hs, hr, cs, cr,
 ):
     f = lax.axis_index("frame")
@@ -326,7 +373,6 @@
     gain_ref[...] = gain
     queries = mm(x_ref[...], sp_ref[...]).astype(BF)
     q_ref[...] = queries
-    qt_ref[...] = queries.T
     grad_z = ct_ref[...].astype(F32) * gain
     grad_zb = grad_z.astype(BF)
     gzb_ref[...] = grad_zb
@@ -351,7 +397,6 @@
     resid_ref[...] = resid
     grad_mixed = mm(resid.astype(BF), op_ref[...], 1, 1).astype(BF)
     do_ref[...] = grad_mixed
-    dot_ref[...] = grad_mixed.T
 
     rim = WMAX * COLS
     start = pl.multiple_of((1 - r) * (tokens - rim), rim)
@@ -389,18 +434,17 @@
     vm = pl.BlockSpec(memory_space=pltpu.VMEM)
     dma = pltpu.SemaphoreType.DMA
     rows = jax.ShapeDtypeStruct((count, width), BF)
-    columns = jax.ShapeDtypeStruct((width, count), BF)
     return pl.pallas_call(
         functools.partial(fetch_kernel, frames),
         out_shape=(
             jax.ShapeDtypeStruct((6, count, width), BF),
             jax.ShapeDtypeStruct((6, WMAX * COLS, width), BF),
-            rows, columns, rows, columns, rows,
+            rows, rows, rows,
             jax.ShapeDtypeStruct((count, width), F32),
             jax.ShapeDtypeStruct((1, width), F32),
         ),
         in_specs=[pl.BlockSpec(memory_space=pltpu.SMEM)] + [vm] * 6,
-        out_specs=(vm,) * 9,
+        out_specs=(vm,) * 7,
         scratch_shapes=[
             pltpu.VMEM((COLS, width), BF),
             pltpu.VMEM((count + 2 * COLS, width), BF),
@@ -648,7 +692,7 @@
         frame_id - 2, frame_id + 2, frame_id + 1 - 2 * odd,
         frame_id - 4, frame_id + 4, frame_id - 1 + 2 * odd,
     )
-    buf, halo, q, qt, do, dot, grad_zb, grad_resid, gain = fetch(
+    buf, halo, q, do, grad_zb, grad_resid, gain = fetch(
         quant_level, tokens, cotangent[0], quant_scale, shared_proj, output_proj, conv_taps, frames
     )
     kinds = jnp.zeros((2,), jnp.int32)
@@ -657,7 +701,7 @@
     rest = jnp.stack([windows[0], row_id, jnp.int32(total_rows)]).astype(jnp.int32)
     meta = jnp.concatenate([kinds, rest])
     residual, hidden, grad_latents, partial, grad_shared, grad_values, grad_output = attention(
-        meta, buf, halo, tokens, q, qt, do, dot, grad_resid, shared_proj, value_proj, output_proj
+        meta, buf, halo, tokens, q, do, grad_resid, shared_proj, value_proj, output_proj
     )
     hidden_ext = row_halo(hidden.reshape(grid), row_id, 1).reshape(-1, width)
     context = residual

time: 103 us -> 89.7 us (0.87)
  Pallas kernels: 85.2 us -> 72 us
    pallas_call x1, Pallas kernels: 28.5 us -> 15.5 us  [attention(): pl.pallas_call(attention_kernel, out_shape=(full, jax.ShapeDtypeStruct((t...]
  transfers between devices with their start and end apart: 2 -> 2, of which waited for: 0 -> 0; matrix products, arithmetic and copies ran while one was open for 5% -> 6% of each run, Pallas kernels for 0% -> 0%
where the time goes in v1:
time: 89.7 us; the launch traced here: 89.2 us
  Pallas kernels  72 us (80%)
  other arithmetic  6.42 us (7%)
  local copies, waits for them, and re-layouts  4.85 us (5%)
  matrix products  3.15 us (4%)
  between operations  2.23 us (2%)
    pallas_call x1, Pallas kernels, reduce(): pl.pallas_call(functools.partial(reduce_kernel, frames), out_shape=(jax.S...  35.8 us
    pallas_call x1, Pallas kernels, fetch(): pl.pallas_call(functools.partial(fetch_kernel, frames), out_shape=(jax.Sh...  20.6 us
    pallas_call x1, Pallas kernels, attention(): pl.pallas_call(attention_kernel, out_shape=(full, jax.ShapeDtypeStruct((t...  15.5 us
    dot_general x6, matrix products, mm(): lax.dot_general(a, b, (((ca,), (cb,)), ((), ())), preferred_element_type=...  3.15 us
    unnamed x30, local copies, waits for them, and re-layouts  3.01 us
  transfers between devices with their start and end apart: 2, of which 0 were waited for; matrix products, arithmetic and copies ran while one was open for 6% of the time, Pallas kernels for 0%

profile of v1, /device:TPU:0, one launch (start us, length us, event | category | flops | bytes accessed | tf_op | source)
XLA Modules:
  0.0 89.2 jit_solution(8287280793314713804)
XLA Ops:
  1.9 0.7 select_select_fusion
  2.6 0.6 pad_add_fusion.meta_ref
  3.2 20.6 %fetch.1 = (bf16[6,512,256]{2,1,0:T(8,128)(2,1)}, bf16[6,128,256]{2,1,0:T(8,128)(2,1)}, bf16[512,256]{1,0:T(8,128)(2,1)}, bf16[512,256]{1,0:T(8,128)(2,1)}, bf16...) custom-call(s32[1]{0:T(128)S(6)} %copy.23.level_ref, bf16[512,256]{1,0:T(8,128)(2,1)} %bitcast.95, ...), custom_call_target="tpu_custom_call" | custom-call | tf_op jit(solution)/shard_map/fetch/pallas_call | solution.py:437
  23.9 0.0 copy-start.11
  23.9 0.0 copy-start.1
  23.9 15.5 %attention.1 = (f32[512,256]{1,0:T(8,128)}, bf16[512,256]{1,0:T(8,128)(2,1)}, f32[512,256]{1,0:T(8,128)}, f32[2,768,256]{2,1,0:T(8,128)}, f32[256,256]{1,0:T(8,1...) custom-call(s32[5]{0:T(128)} %pad_add_fusion.meta_ref, bf16[6,512,256]{2,1,0:T(8,128)(2,1)} %get-tuple-element.22.buf_hbm, ...), custom_call_target="tpu_custom_call" | custom-call | flops 20000000000 | bytes 8000000 | tf_op jit(solution)/shard_map/attention/pallas_call | solution.py:236
  39.4 0.0 copy-start
  39.4 0.0 copy-start.3
  39.4 0.0 copy-start.5
  39.4 0.9 select_bitcast_fusion
  40.3 0.3 collective-permute-start
  40.7 1.1 %fusion.4 = bf16[2,2,64,256]{3,2,1,0:T(8,128)(2,1)S(1)} fusion(f32[2,12,64,256]{3,2,1,0:T(8,128)} %bitcast.84, pred[]{:T(512)S(6)} %eq.115), kind=kLoop, calls=%fused_computation.23 | loop fusion | flops 65536 | bytes 393217 | tf_op jit(solution)/shard_map/convert_element_type | solution.py:715
  41.7 0.2 collective-permute-start.1
  41.9 0.0 copy-done.11
  41.9 0.0 copy-done.1
  42.0 1.2 %convolution_bitcast_fusion.1 = f32[1,256,256]{2,1,0:T(8,128)S(1)} fusion(bf16[512,256]{1,0:T(8,128)(2,1)} %get-tuple-element.28, bf16[512,256]{1,0:T(8,128)(2,1)S(1)} %copy-done.1), kind=kOutput, calls=%fused_computation.8 | convolution fusion | flops 67108864 | bytes 786432 | tf_op jit(solution)/shard_map/dot_general | solution.py:23
  43.2 0.0 collective-permute-done
  43.2 0.0 copy-done
  43.3 0.3 convolution_bitcast_fusion.2
  43.5 0.0 copy-done.3
  43.5 0.0 copy-done.5
  43.6 0.2 convolution_add_fusion.2
  43.8 0.0 copy-start.6
  43.8 0.0 copy-start.7
  43.8 0.0 copy-start.8
  43.8 0.2 convolution_add_fusion.1
  44.1 0.3 convolution_bitcast_fusion
  44.3 0.1 pad_maximum_fusion.1
  44.4 0.3 copy-done.6
  44.7 0.1 copy-done.7
  44.8 0.1 copy-done.8
  44.9 0.0 copy-start.10
  44.9 1.2 %pad_maximum_fusion = f32[1536,256]{1,0:T(8,128)} fusion(f32[768,256]{1,0:T(8,128)S(1)} %bitcast.78, f32[256,256]{1,0:T(8,128)S(1)} %copy-done.8, f32[256,256]{1,0:T(8,128)S(1)} %copy-done.7, f32[256,256]{1,0:T(8,128)S(1)} %copy-done.6), kind=kLoop, calls=%fused_computation | loop fusion | flops 1179648 | bytes 3145728 | tf_op jit(solution)/shard_map/concatenate | solution.py:737
  46.2 0.0 copy-start.4
  46.2 0.0 copy-done.10
  46.2 0.9 %fusion.2 = bf16[1,512,256]{2,1,0:T(8,128)(2,1)} fusion(f32[512,256]{1,0:T(8,128)S(1)} %convolution_add_fusion.1, bf16[512,256]{1,0:T(8,128)(2,1)S(1)} %bitcast.81, f32[256]{0:T(256)S(1)} %bitcast.97, bf16[3,256,256]{2,1,0:T(8,128)(2,1)S(1)} %copy-done.3), kind=kOutput, calls=%fused_computation.10 | convolution fusion | flops 67502080 | bytes 1180672 | tf_op jit(solution)/shard_map/dot_general | solution.py:23
  47.1 0.0 collective-permute-done.1
  47.2 0.5 copy-done.4
  47.7 0.5 select_reduce_fusion
  48.4 0.0 copy-start.2
  48.4 1.1 %copy-done.2 = bf16[6,512,256]{2,1,0:T(8,128)(2,1)} copy-done((bf16[6,512,256]{2,1,0:T(8,128)(2,1)}, bf16[6,512,256]{2,1,0:T(8,128)(2,1)S(1)}, u32[]{:S(2)}) %copy-start.2) | copy-done | bytes 1572888
  49.5 35.8 %reduce.1 = (bf16[512,256]{1,0:T(8,128)(2,1)}, bf16[2,8,96,256]{3,2,1,0:T(8,128)(2,1)}) custom-call(bf16[6,512,256]{2,1,0:T(8,128)(2,1)} %copy-done.2, f32[512,256]{1,0:T(8,128)} %get-tuple-element.31.base_ref, f32[2,8,96,256]{3,2,1,0:T(8,128)} %bitcast.76), custom_call_target="tpu_custom_call" | custom-call | tf_op jit(solution)/shard_map/reduce/pallas_call | solution.py:637
  85.4 1.3 %convert_multiply_fusion = f32[2,8,96,256]{3,2,1,0:T(8,128)S(1)} fusion(bf16[2,8,96,256]{3,2,1,0:T(8,128)(2,1)} %get-tuple-element.37), kind=kLoop, calls=%fused_computation.1 | loop fusion | flops 786432 | bytes 2359296 | tf_op jit(solution)/shard_map/mul | solution.py:743
  86.7 0.0 copy-start.9
  86.7 0.9 %slice.80 = f32[1,8,96,256]{3,2,1,0:T(8,128)} slice(f32[2,8,96,256]{3,2,1,0:T(8,128)S(1)} %convert_multiply_fusion), slice={[1:2], [0:8], [0:96], [0:256]} | slice | bytes 1572864 | tf_op jit(solution)/shard_map/slice | solution.py:750
  87.6 0.9 fusion.11
  88.5 0.0 copy-done.9
  88.5 0.7 copy.24
  (10 shorter events, 0.2 us)
Async XLA Ops:
  23.9 18.1 %copy-start.11 = (s32[1,2]{1,0:T(1,128)S(1)}, s32[1,2]{1,0:T(1,128)}, u32[]{:S(2)}) copy-start(s32[1,2]{1,0:T(1,128)} %param.11) | copy-start | bytes 28
  23.9 18.1 %copy-start.1 = (bf16[512,256]{1,0:T(8,128)(2,1)S(1)}, bf16[512,256]{1,0:T(8,128)(2,1)}, u32[]{:S(2)}) copy-start(bf16[512,256]{1,0:T(8,128)(2,1)} %get-tuple-element.35) | copy-start | bytes 786436
  39.4 3.8 %copy-start = (bf16[512,256]{1,0:T(8,128)(2,1)S(1)}, bf16[512,256]{1,0:T(8,128)(2,1)}, u32[]{:S(2)}) copy-start(bf16[512,256]{1,0:T(8,128)(2,1)} %get-tuple-element.28) | copy-start | bytes 786436
  39.4 4.1 %copy-start.3 = (bf16[3,256,256]{2,1,0:T(8,128)(2,1)S(1)}, bf16[3,256,256]{2,1,0:T(8,128)(2,1)}, u32[]{:S(2)}) copy-start(bf16[3,256,256]{2,1,0:T(8,128)(2,1)} %taps_ref.1) | copy-start | bytes 1179652
  39.4 4.1 %copy-start.5 = (f32[512,256]{1,0:T(8,128)S(1)}, f32[512,256]{1,0:T(8,128)}, u32[]{:S(2)}) copy-start(f32[512,256]{1,0:T(8,128)} %get-tuple-element.27) | copy-start | bytes 1572868
  40.3 2.9 %collective-permute-start = (bf16[1,64,256]{2,1,0:T(8,128)(2,1)S(1)}, bf16[1,64,256]{2,1,0:T(8,128)(2,1)S(1)}, u32[]{:S(2)}, u32[]{:S(2)}) collective-permute-start(bf16[1,64,256]{2,1,0:T(8,128)(2,1)S(1)} %select_bitcast_fusion), channel_id=1, source_target_pairs={{0,1},{1,0},{2,3},{3,2},{4,5},{5,4},{6,7},{7,6},{8,9},{9,8},{10,11... | collective-permute-start | bytes 98312 | tf_op jit(solution)/shard_map/ppermute | solution.py:661
  41.7 5.4 %collective-permute-start.1 = (bf16[2,2,64,256]{3,2,1,0:T(8,128)(2,1)S(1)}, bf16[2,2,64,256]{3,2,1,0:T(8,128)(2,1)S(1)}, u32[]{:S(2)}, u32[]{:S(2)}) collective-permute-start(bf16[2,2,64,256]{3,2,1,0:T(8,128)(2,1)S(1)} %fusion.4), channel_id=1, source_target_pairs={{0,1},{1,0},{2,3},{3,2},{4,5},{5,4},{6,7},{7,6},{8,9},{9,8},{10,11... | collective-permute-start | bytes 393224 | tf_op jit(solution)/shard_map/ppermute | solution.py:661
  43.8 1.0 %copy-start.6 = (f32[256,256]{1,0:T(8,128)S(1)}, f32[256,256]{1,0:T(8,128)}, u32[]{:S(2)}) copy-start(f32[256,256]{1,0:T(8,128)} %get-tuple-element.32) | copy-start | bytes 786436
  43.8 1.0 %copy-start.7 = (f32[256,256]{1,0:T(8,128)S(1)}, f32[256,256]{1,0:T(8,128)}, u32[]{:S(2)}) copy-start(f32[256,256]{1,0:T(8,128)} %get-tuple-element.33) | copy-start | bytes 786436
  43.8 1.1 %copy-start.8 = (f32[256,256]{1,0:T(8,128)S(1)}, f32[256,256]{1,0:T(8,128)}, u32[]{:S(2)}) copy-start(f32[256,256]{1,0:T(8,128)} %get-tuple-element.34) | copy-start | bytes 786436
  44.9 1.3 %copy-start.10 = (f32[1,256]{1,0:T(1,128)S(1)}, f32[1,256]{1,0:T(1,128)}, u32[]{:S(2)}) copy-start(f32[1,256]{1,0:T(1,128)} %get-tuple-element.29) | copy-start | bytes 3076
  46.2 1.5 %copy-start.4 = (f32[2,768,256]{2,1,0:T(8,128)S(1)}, f32[2,768,256]{2,1,0:T(8,128)}, u32[]{:S(2)}) copy-start(f32[2,768,256]{2,1,0:T(8,128)} %get-tuple-element.30) | copy-start | bytes 4718596
  48.4 1.2 %copy-start.2 = (bf16[6,512,256]{2,1,0:T(8,128)(2,1)}, bf16[6,512,256]{2,1,0:T(8,128)(2,1)S(1)}, u32[]{:S(2)}) copy-start(bf16[6,512,256]{2,1,0:T(8,128)(2,1)S(1)} %bitcast_dynamic-update-slice_fusion.out_ref) | copy-start | bytes 4718596
  86.7 1.8 %copy-start.9 = (bf16[512,256]{1,0:T(8,128)(2,1)S(1)}, bf16[512,256]{1,0:T(8,128)(2,1)}, u32[]{:S(2)}) copy-start(bf16[512,256]{1,0:T(8,128)(2,1)} %get-tuple-element.36) | copy-start | bytes 786436

commit v2 on v1

v2 whole, which is shorter than its diff:
```python
import functools
import math

import jax
import jax.numpy as jnp
from jax import lax
from jax.experimental import pallas as pl
from jax.experimental.pallas import tpu as pltpu
from jax.sharding import PartitionSpec as P

HEADS = 8
DH = 32
COLS = 64
WMAX = 2
RING = 3
KINDS = 6

SCORE_SCALE = 1.5 / math.sqrt(DH)
LOG2E = math.log2(math.e)
BF = jnp.bfloat16
F32 = jnp.float32
MESH = pl.DeviceIdType.MESH


def mm(a, b, ca=1, cb=0):
    return lax.dot_general(a, b, (((ca,), (cb,)), ((), ())), preferred_element_type=F32)


HALF = 4


def masked_rows(block, f0):
    lane = lax.broadcasted_iota(jnp.int32, (1, HALF * DH), 1) // DH
    part = block[:, f0 : f0 + HALF * DH]
    return jnp.concatenate(
        [jnp.where(lane == h, part, jnp.zeros_like(part)) for h in range(HALF)], axis=0
    )


def head_diagonal(wide):
    rows = wide.T
    lane = lax.broadcasted_iota(jnp.int32, (1, HALF * DH), 1) // DH
    out = rows[:COLS]
    for h in range(1, HALF):
        out = jnp.where(lane == h, rows[h * COLS : (h + 1) * COLS], out)
    return out


def forward_row(i, bias, k_ref, qm_ref, p_ref, pb_ref, inv_ref):
    band = 2 * COLS
    reach = 2 * WMAX + 1
    wide = HALF * COLS
    base = i * band
    kk = SCORE_SCALE * LOG2E
    for hf in range(2):
        f0 = hf * HALF * DH
        ft = slice(f0, f0 + HALF * DH)
        p_ref[i, hf] = mm(k_ref[base : base + reach * band, ft], qm_ref[i, hf], 1, 1)
        m8 = None
        for c in range(reach):
            x = p_ref[i, hf, c * band : (c + 1) * band, :].reshape(band // 8, 8, wide)
            top = jnp.max(x, axis=0) + bias[c]
            m8 = top if m8 is None else jnp.maximum(m8, top)
        m = jnp.max(m8, axis=0, keepdims=True)
        l8 = jnp.zeros((8, wide), F32)
        for c in range(reach):
            sl = slice(c * band, (c + 1) * band)
            p = jnp.exp2(p_ref[i, hf, sl, :] * kk + (bias[c] - m) * kk)
            p_ref[i, hf, sl, :] = p
            l8 = l8 + jnp.sum(p.reshape(band // 8, 8, wide), axis=0)
        inv = 1.0 / jnp.sum(l8, axis=0, keepdims=True)
        inv_ref[i, hf] = inv
        for c in range(reach):
            sl = slice(c * band, (c + 1) * band)
            pb_ref[i, hf, sl, :] = (p_ref[i, hf, sl, :] * inv).astype(BF)


def mix_row(i, vt_ref, pb_ref, mix_ref):
    band = 2 * COLS
    reach = 2 * WMAX + 1
    base = i * band
    for hf in range(2):
        f0 = hf * HALF * DH
        ft = slice(f0, f0 + HALF * DH)
        mix = mm(vt_ref[ft, base : base + reach * band], pb_ref[i, hf])
        mix_ref[i * COLS : (i + 1) * COLS, ft] = head_diagonal(mix).astype(BF)


def score_row(i, v_ref, dom_ref, p_ref, inv_ref, dp_ref, ds_ref):
    band = 2 * COLS
    reach = 2 * WMAX + 1
    wide = HALF * COLS
    base = i * band
    win = slice(base, base + reach * band)
    for hf in range(2):
        f0 = hf * HALF * DH
        ft = slice(f0, f0 + HALF * DH)
        dp_ref[i % RING, hf] = mm(v_ref[win, ft], dom_ref[i, hf], 1, 1)
        u8 = jnp.zeros((8, wide), F32)
        for c in range(reach):
            sl = slice(c * band, (c + 1) * band)
            x = p_ref[i, hf, sl, :] * dp_ref[i % RING, hf, sl, :]
            u8 = u8 + jnp.sum(x.reshape(band // 8, 8, wide), axis=0)
        inv = inv_ref[i, hf]
        ci = inv * SCORE_SCALE
        inner = jnp.sum(u8, axis=0, keepdims=True) * inv * ci
        for c in range(reach):
            sl = slice(c * band, (c + 1) * band)
            ds_ref[i % RING, hf, sl, :] = (p_ref[i, hf, sl, :] * (dp_ref[i % RING, hf, sl, :] * ci - inner)).astype(BF)


def query_row(i, kt_ref, ds_ref, dq_ref):
    band = 2 * COLS
    base = i * band
    win = slice(base, base + (2 * WMAX + 1) * band)
    for hf in range(2):
        f0 = hf * HALF * DH
        ft = slice(f0, f0 + HALF * DH)
        dq = mm(kt_ref[ft, win], ds_ref[i % RING, hf])
        dq_ref[i * COLS : (i + 1) * COLS, ft] = head_diagonal(dq).astype(BF)


def key_row(i, qm_ref, dom_ref, pb_ref, ds_ref, dk_ref, dv_ref):
    band = 2 * COLS
    base = i * band
    win = slice(base, base + (2 * WMAX + 1) * band)
    for hf in range(2):
        f0 = hf * HALF * DH
        ft = slice(f0, f0 + HALF * DH)
        dk_ref[win, ft] += mm(ds_ref[i % RING, hf], qm_ref[i, hf])
        dv_ref[win, ft] += mm(pb_ref[i, hf], dom_ref[i, hf])


def loop(first, last, body):
    lax.fori_loop(first, last, lambda k, carry: (body(k), carry)[1], 0)


class Sum:
    def __init__(self, refs, f, r, frames):
        (self.w, self.p, self.xs, self.xr, self.zw, self.zs, self.zr, self.res,
         self.one, self.zss, self.zsr, self.gs, self.gr) = refs
        self.n = frames // 2
        self.r, self.odd, self.me = r, lax.rem(f, 2), f // 2
        self.across = {"frame": f + 1 - 2 * self.odd}
        self.partner = {"row": 1 - r}

    def link(self, i, source, target, device):
        return pltpu.make_async_remote_copy(
            source, target, self.one.at[2 * i], self.one.at[2 * i + 1],
            device_id=device, device_id_type=MESH,
        )

    def pair(self):
        return self.link(0, self.w.at[1 - self.r], self.p, self.partner)

    def cross(self):
        return self.link(1, self.xs, self.xr, self.across)

    def cross_back(self):
        part = self.res.at[self.r, self.odd]
        return self.link(2, part, part, self.across)

    def pair_back(self, i):
        side = self.odd if i == 0 else 1 - self.odd
        part = self.res.at[self.r, side]
        return self.link(3 + i, part, part, self.partner)

    def scatter(self, k, incoming):
        other = lax.rem(self.me + k, self.n)
        if incoming:
            return pltpu.make_async_remote_copy(
                self.zs.at[other], self.zr.at[other], self.zss.at[k], self.zsr.at[other],
                device_id={"frame": 2 * other + self.odd}, device_id_type=MESH,
            )
        return pltpu.make_async_remote_copy(
            self.zs.at[other], self.zr.at[self.me], self.zss.at[k], self.zsr.at[self.me],
            device_id={"frame": 2 * other + self.odd}, device_id_type=MESH,
        )

    def gather(self, k, incoming):
        other = lax.rem(self.me + k, self.n)
        slot = other if incoming else self.me
        part = self.res.at[self.r, self.odd, slot]
        return pltpu.make_async_remote_copy(
            part, part, self.gs.at[k], self.gr.at[slot],
            device_id={"frame": 2 * other + self.odd}, device_id_type=MESH,
        )

    def begin(self):
        self.pair().start()

    def send_cross(self):
        self.pair().wait()
        away = 1 - self.odd
        self.xs[...] = (self.w[self.r, away] + self.p[away]).astype(BF)
        self.cross().start()

    def send_pieces(self):
        self.cross().wait()
        total = self.w[self.r, self.odd] + self.p[self.odd] + self.xr[...].astype(F32)
        size = total.shape[0] // self.n
        for j in range(self.n):
            piece = total[j * size : (j + 1) * size]
            self.zw[j] = piece
            self.zs[j] = piece.astype(BF)
        loop(1, self.n, lambda k: self.scatter(k, False).start())

    def send_totals(self):
        def add(k, total):
            self.scatter(k, True).wait_recv()
            return total + self.zr[lax.rem(self.me + k, self.n)].astype(F32)

        total = lax.fori_loop(1, self.n, add, self.zw[self.me])
        self.res[self.r, self.odd, self.me] = total.astype(BF)
        loop(1, self.n, lambda k: self.gather(k, False).start())

    def send_back(self):
        loop(1, self.n, lambda k: self.gather(k, True).wait_recv())
        self.cross_back().start()
        self.pair_back(0).start()

    def send_other(self):
        self.cross_back().wait_recv()
        self.pair_back(1).start()

    def finish(self):
        self.pair_back(0).wait()
        self.pair_back(1).wait()
        self.cross_back().wait_send()

        def sent(k):
            self.scatter(k, False).wait_send()
            self.gather(k, False).wait_send()

        loop(1, self.n, sent)

    def quarter(self, half, side):
        return jnp.concatenate(
            [self.res[half, side, j].astype(F32) for j in range(self.n)], axis=0
        )


def codec_kernel(
    frames, refs_ref, window_ref, level_ref, x_ref, ct_ref, qs_ref, sp_ref, vp_ref, op_ref, taps_ref,
    coded_ref, lat_ref, gs_ref, gv_ref, go_ref, gt_ref,
    buf_ref, halo_ref, q_ref, do_ref, gp_ref, resid_ref, cth_ref, ext_ref,
    xi_ref, k_ref, v_ref, kt_ref, vt_ref, mix_ref, dq_ref, dk_ref, dv_ref,
    p_ref, pb_ref, inv_ref, dp_ref, ds_ref, qm_ref, dom_ref,
    residual_ref, hx_ref, eh_ref, ph_ref, pg_ref, out_ref, rb_ref, sb_ref,
    ssem, rsem, hs, hr, bs, br, one,
    *sums,
):
    f = lax.axis_index("frame")
    r = lax.axis_index("row")
    tokens, width = x_ref.shape
    rows = tokens // COLS
    rim = WMAX * COLS
    step = rim
    chunks = tokens // step
    total_rows = rows * lax.axis_size("row")
    odd = lax.rem(f, 2)
    pair = f + 1 - 2 * odd
    lo2, hi2, lo4, hi4 = f >= 2, f + 2 < frames, f >= 4, f + 4 < frames
    side = ((odd == 1) & (f + 1 < frames)) | ((odd == 0) & (f >= 1))
    relay = ((odd == 1) & lo2) | ((odd == 0) & hi2)
    always = f >= 0
    partner = {"row": 1 - r}
    up, down, across = {"frame": f + 2}, {"frame": f - 2}, {"frame": pair}
    weights = Sum(sums[:13], f, r, frames)
    projections = Sum(sums[13:], f, r, frames)

    barrier = pltpu.get_barrier_semaphore()
    pl.semaphore_signal(barrier, inc=1, device_id=partner, device_id_type=MESH)
    pl.semaphore_signal(barrier, inc=1, device_id=across, device_id_type=MESH)

    def hello(k):
        other = {"frame": lax.rem(f + 2 * k, frames)}
        pl.semaphore_signal(barrier, inc=1, device_id=other, device_id_type=MESH)

    loop(1, frames // 2, hello)
    pl.semaphore_wait(barrier, frames // 2 + 1)

    def link(i, source, target, device):
        return pltpu.make_async_remote_copy(
            source, target, one.at[2 * i], one.at[2 * i + 1],
            device_id=device, device_id_type=MESH,
        )

    def place(c):
        return pl.multiple_of(jnp.where(r == 0, chunks - 1 - c, c) * step, step)

    edge = pl.multiple_of((1 - r) * (tokens - COLS), COLS)
    ct_copy = link(0, ct_ref.at[pl.ds(edge, COLS)], cth_ref, partner)
    ct_copy.start()

    def copy(kind, c, source, device):
        part = pl.ds(place(c), step)
        return pltpu.make_async_remote_copy(
            source.at[part], buf_ref.at[kind, part], ssem.at[kind, c], rsem.at[kind, c],
            device_id=device, device_id_type=MESH,
        )

    def halo(kind):
        return pltpu.make_async_remote_copy(
            buf_ref.at[kind, pl.ds(place(0), rim)], halo_ref.at[kind], hs.at[kind], hr.at[kind],
            device_id=partner, device_id_type=MESH,
        )

    have = (lo2, hi2, always, lo4, hi4, side)
    for c in range(chunks):

        @pl.when(hi2)
        def _():
            copy(0, c, x_ref, up).start()

        @pl.when(lo2)
        def _():
            copy(1, c, x_ref, down).start()

        copy(2, c, x_ref, across).start()

    def pass_on(c):
        @pl.when(lo2)
        def _():
            copy(0, c, x_ref, across).wait_recv()
            if c == 0:
                halo(0).start()

        @pl.when(lo2 & hi2)
        def _():
            copy(3, c, buf_ref.at[0], up).start()

        @pl.when(lo2 & (odd == 1))
        def _():
            copy(5, c, buf_ref.at[0], across).start()

        @pl.when(hi2)
        def _():
            copy(1, c, x_ref, across).wait_recv()
            if c == 0:
                halo(1).start()

        @pl.when(hi2 & lo2)
        def _():
            copy(4, c, buf_ref.at[1], down).start()

        @pl.when(hi2 & (odd == 0))
        def _():
            copy(5, c, buf_ref.at[1], across).start()

    level = lax.broadcasted_iota(jnp.int32, (qs_ref.shape[0], 1), 0)
    gain = jnp.sum(
        jnp.where(level == level_ref[0], qs_ref[...], 0.0), axis=0, keepdims=True
    )
    q_ref[...] = mm(x_ref[...], sp_ref[...]).astype(BF)
    grad_z = ct_ref[...].astype(F32) * gain
    resid_ref[...] = grad_z
    grad_zb = grad_z.astype(BF)
    gp_ref[: 2 * COLS, :] = jnp.zeros((2 * COLS, width), BF)
    gp_ref[2 * COLS : 2 * COLS + tokens, :] = grad_zb
    gp_ref[2 * COLS + tokens :, :] = jnp.zeros((2 * COLS, width), BF)
    ext_ref[COLS : COLS + tokens, :] = grad_zb
    dk_ref[...] = jnp.zeros_like(dk_ref)
    dv_ref[...] = jnp.zeros_like(dv_ref)
    got = (lo2, hi2, always, lo2 & hi2, lo2 & hi2, relay)
    for kind in (0, 1, 3, 4, 5):

        @pl.when(jnp.logical_not(got[kind]))
        def _():
            rb_ref[kind, :, :] = jnp.zeros((tokens, width), BF)

    ct_copy.wait()
    outer = (cth_ref[...].astype(F32) * gain).astype(BF)
    blank = jnp.zeros_like(outer)
    ext_ref[:COLS, :] = jnp.where(r == 0, blank, outer)
    ext_ref[COLS + tokens :, :] = jnp.where(r == 0, outer, blank)
    pass_on(0)
    resid = resid_ref[...]
    for t in range(3):
        resid = resid + mm(ext_ref[(2 - t) * COLS : (2 - t) * COLS + tokens, :], taps_ref[t], 1, 1)
    resid_ref[...] = resid
    pass_on(1)
    do_ref[...] = mm(resid_ref[...].astype(BF), op_ref[...], 1, 1).astype(BF)
    copy(2, 0, x_ref, across).wait_recv()
    halo(2).start()
    for c in range(2, chunks):
        pass_on(c)
    for i in range(rows):
        tok = slice(i * COLS, (i + 1) * COLS)
        for hf in range(2):
            qm_ref[i, hf] = masked_rows(q_ref[tok, :], hf * HALF * DH)
            dom_ref[i, hf] = masked_rows(do_ref[tok, :], hf * HALF * DH)
    for c in range(chunks):
        for kind in range(2, KINDS):
            if kind > 2 or c:

                @pl.when(have[kind])
                def _():
                    copy(kind, c, x_ref, across).wait_recv()
                    if c == 0:
                        halo(kind).start()

    for kind in range(KINDS):

        @pl.when(have[kind])
        def _():
            halo(kind).wait()

    sources = (f - 2, f + 2, pair, f - 4, f + 4, f - 1 + 2 * odd)
    targets = (f + 2, f - 2, pair, f + 4, f - 4, f - 1 + 2 * odd)
    for s in range(2):
        own = refs_ref[0, s]
        kind = jnp.int32(0)
        for number, source in enumerate(sources):
            kind = jnp.where(own == source, number, kind)
        for e in range(rows):
            at = (2 * (e + WMAX) + s) * COLS
            xi_ref[at : at + COLS, :] = buf_ref[kind, e * COLS : (e + 1) * COLS, :]
        for e in range(WMAX):
            piece = halo_ref[kind, e * COLS : (e + 1) * COLS, :]
            none = jnp.zeros_like(piece)
            at = (2 * e + s) * COLS
            xi_ref[at : at + COLS, :] = jnp.where(r == 0, none, piece)
            at = (2 * (e + WMAX + rows) + s) * COLS
            xi_ref[at : at + COLS, :] = jnp.where(r == 0, piece, none)

    keys = mm(xi_ref[...], sp_ref[...]).astype(BF)
    k_ref[...] = keys
    kt_ref[...] = keys.T
    vals = mm(xi_ref[...], vp_ref[...]).astype(BF)
    v_ref[...] = vals
    vt_ref[...] = vals.T
    first_row = r * rows
    window = window_ref[0]

    def bias_of(i):
        out = []
        for c in range(2 * WMAX + 1):
            key_row = first_row + i + c - WMAX
            inside = (key_row >= 0) & (key_row < total_rows) & (abs(c - WMAX) <= window)
            out.append(jnp.where(inside, 0.0, -jnp.inf).astype(F32))
        return out

    for i in range(rows):
        forward_row(i, bias_of(i), k_ref, qm_ref, p_ref, pb_ref, inv_ref)
    for i in range(rows):
        mix_row(i, vt_ref, pb_ref, mix_ref)

    residual = x_ref[...].astype(F32) + mm(mix_ref[...], op_ref[...])
    residual_ref[...] = residual
    hx_ref[COLS : COLS + tokens, :] = residual.astype(BF)
    inner = pl.multiple_of(COLS + (1 - r) * (tokens - COLS), COLS)
    hidden_copy = link(1, hx_ref.at[pl.ds(inner, COLS)], eh_ref, partner)
    hidden_copy.start()
    weights.w[0, 0] = mm(mix_ref[...].T, resid_ref[...].astype(BF))
    hidden_copy.wait()
    outer = eh_ref[...]
    blank = jnp.zeros_like(outer)
    hx_ref[:COLS, :] = jnp.where(r == 0, blank, outer)
    hx_ref[COLS + tokens :, :] = jnp.where(r == 0, outer, blank)
    hxt = hx_ref[...].T
    span = tokens + 2 * COLS
    for t in range(3):
        weights.w[(t + 1) // 2, (t + 1) % 2] = mm(hxt, gp_ref[(2 - t) * COLS : (2 - t) * COLS + span, :])
    weights.begin()

    for i in range(rows + 1):
        if i == 2:
            weights.send_cross()
        if i == 6:
            weights.send_pieces()
        if i < rows:
            score_row(i, v_ref, dom_ref, p_ref, inv_ref, dp_ref, ds_ref)
        if i:
            key_row(i - 1, qm_ref, dom_ref, pb_ref, ds_ref, dk_ref, dv_ref)
            query_row(i - 1, kt_ref, ds_ref, dq_ref)

    def project(at):
        return mm(dk_ref[pl.ds(at, 2 * step), :].astype(BF), sp_ref[...], 1, 1) + mm(
            dv_ref[pl.ds(at, 2 * step), :].astype(BF), vp_ref[...], 1, 1
        )

    ph_ref[...] = project(
        pl.multiple_of(jnp.where(r == 0, 2 * (tokens + rim), 0), 2 * step)
    ).astype(BF)
    part_copy = link(2, ph_ref, pg_ref, partner)
    part_copy.start()

    sent = (hi2, lo2, always, hi4, lo4, side)
    device = (up, down, across, up, down, across)

    def give(kind, c, source):
        part = pl.ds(place(c), step)
        return pltpu.make_async_remote_copy(
            source.at[part], rb_ref.at[kind, part], bs.at[kind, c], br.at[kind, c],
            device_id=device[kind], device_id_type=MESH,
        )

    def hand_out(c):
        at = place(c)
        block = project(pl.multiple_of(2 * at + 2 * rim, 2 * step))
        if c == 0:
            block = block + pg_ref[...].astype(F32)
        for kind, target in enumerate(targets):
            first = refs_ref[0, 0] == target
            second = refs_ref[0, 1] == target
            for e in range(WMAX):
                part = jnp.where(first, block[2 * e * COLS : (2 * e + 1) * COLS], 0.0)
                part = part + jnp.where(second, block[(2 * e + 1) * COLS : (2 * e + 2) * COLS], 0.0)
                out_ref[kind, pl.ds(pl.multiple_of(at + e * COLS, COLS), COLS), :] = part.astype(BF)
        for kind in (3, 4, 5, 2):

            @pl.when(sent[kind])
            def _():
                give(kind, c, out_ref.at[kind]).start()

    even = jnp.where(odd == 0, 1.0, 0.0).astype(F32)

    def merge(c):
        for kind in (3, 4, 5):

            @pl.when(got[kind])
            def _():
                give(kind, c, out_ref.at[kind]).wait_recv()

        part = pl.ds(place(c), step)
        extra = rb_ref[5, part, :].astype(F32)
        rising = out_ref[0, part, :].astype(F32) + rb_ref[3, part, :].astype(F32) + extra * even
        falling = (
            out_ref[1, part, :].astype(F32) + rb_ref[4, part, :].astype(F32) + extra * (1.0 - even)
        )
        sb_ref[0, part, :] = rising.astype(BF)
        sb_ref[1, part, :] = falling.astype(BF)

        @pl.when(hi2)
        def _():
            give(0, c, sb_ref.at[0]).start()

        @pl.when(lo2)
        def _():
            give(1, c, sb_ref.at[1]).start()

    def collect(c):
        for kind in (0, 1, 2):

            @pl.when(got[kind])
            def _():
                give(kind, c, out_ref.at[kind]).wait_recv()

        part = pl.ds(place(c), step)
        lat_ref[part, :] = (
            resid_ref[part, :]
            + rb_ref[0, part, :].astype(F32)
            + rb_ref[1, part, :].astype(F32)
            + rb_ref[2, part, :].astype(F32)
        ).astype(BF)

    order = tuple(reversed(range(chunks)))
    for c in order[:-1]:
        hand_out(c)
    part_copy.wait()
    hand_out(0)
    weights.send_totals()
    xit = xi_ref[...].T
    grad_shared = mm(x_ref[...].T, dq_ref[...]) + mm(xit, dk_ref[...].astype(BF))
    grad_values = mm(xit, dv_ref[...].astype(BF))
    half = width // 2
    for s in range(2):
        projections.w[0, s] = grad_shared[s * half : (s + 1) * half]
        projections.w[1, s] = grad_values[s * half : (s + 1) * half]
    projections.begin()
    merge(order[0])
    projections.send_cross()
    merge(order[1])
    weights.send_back()
    resid_ref[...] = resid_ref[...] + mm(dq_ref[...], sp_ref[...], 1, 1)
    context = residual_ref[...]
    for t in range(3):
        context = context + mm(hx_ref[t * COLS : t * COLS + tokens, :], taps_ref[t])
    coded_ref[...] = (context * gain).astype(BF)
    projections.send_pieces()
    merge(order[2])
    weights.send_other()
    projections.send_totals()
    for c in order[3:]:
        merge(c)
    projections.send_back()
    norm = 1.0 / math.sqrt(frames * total_rows * COLS)
    for c in order[:2]:
        collect(c)
    projections.send_other()
    weights.finish()
    go_ref[...] = weights.quarter(0, 0) * norm
    for t in range(3):
        gt_ref[t] = weights.quarter((t + 1) // 2, (t + 1) % 2) * norm
    for c in order[2:]:
        collect(c)
    projections.finish()
    for s in range(2):
        gs_ref[s * half : (s + 1) * half, :] = projections.quarter(0, s) * norm
        gv_ref[s * half : (s + 1) * half, :] = projections.quarter(1, s) * norm

    passed = (hi2, lo2, always, lo2 & hi2, lo2 & hi2, relay)
    for kind in range(KINDS):

        @pl.when(passed[kind])
        def _():
            for c in range(chunks):
                copy(kind, c, x_ref, across).wait_send()

        @pl.when(sent[kind])
        def _():
            for c in range(chunks):
                give(kind, c, out_ref.at[kind]).wait_send()


def sum_scratch(size, width, n):
    dma = pltpu.SemaphoreType.DMA
    return [
        pltpu.VMEM((2, 2, size, width), F32),
        pltpu.VMEM((2, size, width), F32),
        pltpu.VMEM((size, width), BF),
        pltpu.VMEM((size, width), BF),
        pltpu.VMEM((n, size // n, width), F32),
        pltpu.VMEM((n, size // n, width), BF),
        pltpu.VMEM((n, size // n, width), BF),
        pltpu.VMEM((2, 2, n, size // n, width), BF),
        dma((10,)), dma((n,)), dma((n,)), dma((n,)), dma((n,)),
    ]


def local(
    latents, ref_frames, windows, quant_level, quant_scale,
    shared_proj, value_proj, output_proj, conv_taps, cotangent,
):
    tokens, width = latents.shape[1:]
    frames = lax.axis_size("frame")
    rows = tokens // COLS
    ext = tokens + 2 * WMAX * COLS
    keys = 2 * (2 * WMAX + 1) * COLS
    wide = HALF * COLS
    rim = WMAX * COLS
    chunks = tokens // rim
    vm = pl.BlockSpec(memory_space=pltpu.VMEM)
    sm = pl.BlockSpec(memory_space=pltpu.SMEM)
    dma = pltpu.SemaphoreType.DMA
    slab = jax.ShapeDtypeStruct((tokens, width), BF)
    square = jax.ShapeDtypeStruct((width, width), F32)

    def rows_of(count, kind=BF):
        return pltpu.VMEM((count, width), kind)

    coded, grad_latents, grad_shared, grad_values, grad_output, grad_taps = pl.pallas_call(
        functools.partial(codec_kernel, frames),
        out_shape=(
            slab, slab, square, square, square, jax.ShapeDtypeStruct((3, width, width), F32),
        ),
        in_specs=[sm] * 3 + [vm] * 7,
        out_specs=(vm,) * 6,
        scratch_shapes=[
            pltpu.VMEM((KINDS, tokens, width), BF),
            pltpu.VMEM((KINDS, rim, width), BF),
            rows_of(tokens), rows_of(tokens), rows_of(tokens + 4 * COLS), rows_of(tokens, F32),
            rows_of(COLS), rows_of(tokens + 2 * COLS),
            rows_of(2 * ext), rows_of(2 * ext), rows_of(2 * ext),
            pltpu.VMEM((width, 2 * ext), BF),
            pltpu.VMEM((width, 2 * ext), BF),
            rows_of(tokens), rows_of(tokens), rows_of(2 * ext, F32), rows_of(2 * ext, F32),
            pltpu.VMEM((rows, 2, keys, wide), F32),
            pltpu.VMEM((rows, 2, keys, wide), BF),
            pltpu.VMEM((rows, 2, 1, wide), F32),
            pltpu.VMEM((RING, 2, keys, wide), F32),
            pltpu.VMEM((RING, 2, keys, wide), BF),
            pltpu.VMEM((rows, 2, wide, HALF * DH), BF),
            pltpu.VMEM((rows, 2, wide, HALF * DH), BF),
            rows_of(tokens, F32), rows_of(tokens + 2 * COLS), rows_of(COLS),
            rows_of(2 * rim), rows_of(2 * rim),
            pltpu.VMEM((KINDS, tokens, width), BF),
            pltpu.VMEM((KINDS, tokens, width), BF),
            pltpu.VMEM((2, tokens, width), BF),
            dma((KINDS, chunks)), dma((KINDS, chunks)), dma((KINDS,)), dma((KINDS,)),
            dma((KINDS, chunks)), dma((KINDS, chunks)), dma((6,)),
        ]
        + sum_scratch(width, width, frames // 2)
        + sum_scratch(width // 2, width, frames // 2),
        compiler_params=pltpu.CompilerParams(
            collective_id=0, has_side_effects=True, vmem_limit_bytes=62_000_000
        ),
        name="codec",
    )(
        ref_frames, windows, quant_level, latents[0], cotangent[0], quant_scale,
        shared_proj, value_proj, output_proj, conv_taps,
    )
    return (
        coded[None], grad_latents[None], grad_shared, grad_values, grad_output, grad_taps
    )


def solution(mesh):
    tok = P(("groups", "frame"), "row", None)
    frm = P(("groups", "frame"))
    placed = (tok, P(("groups", "frame"), None), frm, frm, P(), P(), P(), P(), P(), tok)
    return jax.shard_map(
        local,
        mesh=mesh,
        in_specs=placed,
        out_specs=(
            tok, tok, P("groups", None), P("groups", None), P("groups", None),
            P("groups", None, None),
        ),
        check_vma=False,
    )
```

time: 89.7 us -> 72.6 us (0.81)
  Pallas kernels: 72 us -> 64.3 us
  other arithmetic: 6.42 us -> 0 us
  matrix products: 3.15 us -> 0 us
  local copies, waits for them, and re-layouts: 4.85 us -> 6.09 us
    pallas_call x3 -> x1, Pallas kernels: 72 us -> 64.3 us  [local(): pl.pallas_call(functools.partial(codec_kernel, frames), out_shape=(slab,...]
    dot_general x6 -> x0, matrix products: 3.15 us -> none  [mm(): lax.dot_general(a, b, (((ca,), (cb,)), ((), ())), preferred_element_type=...]
    unnamed x30 -> x16, local copies, waits for them, and re-layouts: 3.01 us -> 6.09 us
    concatenate x3 -> x0, other arithmetic: 1.88 us -> none  [the longest x1 1.25 us: local(): jnp.concatenate([grad_shared, grad_values, grad_output, grad_taps.reshape...]
    slice x2 -> x0, local copies, waits for them, and re-layouts: 1.82 us -> none  [the longest x1 0.93 us: local(): summed[3 * width:].reshape(3, width, width)]
    select_n x4 -> x0, other arithmetic: 1.59 us -> none  [the longest x1 0.87 us: row_halo(): got = from_partner(jnp.where(row_id == 0, last, first))]
    mul x1 -> x0, other arithmetic: 1.3 us -> none  [local(): summed = summed.reshape(-1, width).astype(F32) * norm]
    convert_element_type x1 -> x0, other arithmetic: 1.06 us -> none  [local(): jnp.where(row_id == 0, lower, upper).astype(BF)]
  transfers between devices with their start and end apart: 2 -> 0, of which waited for: 0 -> 0; matrix products, arithmetic and copies ran while one was open for 6% -> 0% of each run, Pallas kernels for 0% -> 0%
where the time goes in v2:
time: 72.6 us; the launch traced here: 72.4 us
  Pallas kernels  64.3 us (89%)
  local copies, waits for them, and re-layouts  6.09 us (8%)
  between operations  1.95 us (3%)
    pallas_call x1, Pallas kernels, local(): pl.pallas_call(functools.partial(codec_kernel, frames), out_shape=(slab,...  64.3 us
    unnamed x16, local copies, waits for them, and re-layouts  6.09 us

profile of v2, /device:TPU:0, one launch (start us, length us, event | category | flops | bytes accessed | tf_op | source)
XLA Modules:
  0.0 72.4 jit_solution(3110824567392904407)
XLA Ops:
  1.9 64.3 %codec.1 = (bf16[512,256]{1,0:T(8,128)(2,1)}, bf16[512,256]{1,0:T(8,128)(2,1)}, f32[256,256]{1,0:T(8,128)}, f32[256,256]{1,0:T(8,128)}, f32[256,256]{1,0:T(8,128)}, /*index=5*/f32[3,256,256]{2,1,0:T(8,128)}) custom-call(s32[1,2]{1,0:T(1,128)} %refs_ref.1, s32[1]{0:T(128)S(6)} %copy.22.window_ref, s32[1]{0:T(128)S(6)} %copy.23.level_ref, ...), custom_call_target="tpu_custom_call" | custom-call | tf_op jit(solution)/shard_map/codec/pallas_call | solution.py:653
  66.3 0.0 copy-start.4
  66.3 1.7 %copy.24 = bf16[1,512,256]{2,1,0:T(8,128)(2,1)} copy(bf16[1,512,256]{2,1,0:T(8,128)(2,1)} %bitcast.5) | data formatting | bytes 524288
  68.0 0.0 copy-done.4
  68.0 0.0 copy-start.3
  68.0 0.0 copy-start.2
  68.0 0.7 copy.25
  68.7 0.3 copy-done.3
  69.0 0.0 copy-start
  69.0 0.7 copy.26
  69.7 0.0 copy-done.2
  69.7 0.0 copy-start.1
  69.7 0.7 copy.27
  70.4 0.3 copy-done.1
  70.8 0.7 copy.28
  71.5 0.0 copy-done
  71.5 0.9 %copy.29 = f32[3,256,256]{2,1,0:T(8,128)} copy(f32[3,256,256]{2,1,0:T(8,128)S(1)} %copy-done) | data formatting | bytes 1572864
Async XLA Ops:
  66.3 1.7 %copy-start.4 = (bf16[512,256]{1,0:T(8,128)(2,1)S(1)}, bf16[512,256]{1,0:T(8,128)(2,1)}, u32[]{:S(2)}) copy-start(bf16[512,256]{1,0:T(8,128)(2,1)} %get-tuple-element.13) | copy-start | bytes 786436
  68.0 1.0 %copy-start.3 = (f32[256,256]{1,0:T(8,128)S(1)}, f32[256,256]{1,0:T(8,128)}, u32[]{:S(2)}) copy-start(f32[256,256]{1,0:T(8,128)} %get-tuple-element.26) | copy-start | bytes 786436
  68.0 1.8 %copy-start.2 = (f32[256,256]{1,0:T(8,128)S(1)}, f32[256,256]{1,0:T(8,128)}, u32[]{:S(2)}) copy-start(f32[256,256]{1,0:T(8,128)} %get-tuple-element.27) | copy-start | bytes 786436
  69.0 2.5 %copy-start = (f32[3,256,256]{2,1,0:T(8,128)S(1)}, f32[3,256,256]{2,1,0:T(8,128)}, u32[]{:S(2)}) copy-start(f32[3,256,256]{2,1,0:T(8,128)} %get-tuple-element.29) | copy-start | bytes 2359300
  69.7 1.0 %copy-start.1 = (f32[256,256]{1,0:T(8,128)S(1)}, f32[256,256]{1,0:T(8,128)}, u32[]{:S(2)}) copy-start(f32[256,256]{1,0:T(8,128)} %get-tuple-element.28) | copy-start | bytes 786436

commit v3 on v2

--- a/solution.py
+++ b/solution.py
@@ -136,9 +136,10 @@
 
 
 class Sum:
-    def __init__(self, refs, f, r, frames):
-        (self.w, self.p, self.xs, self.xr, self.zw, self.zs, self.zr, self.res,
+    def __init__(self, refs, res, f, r, frames):
+        (self.w, self.p, self.xs, self.xr, self.zw, self.zs, self.zr,
          self.one, self.zss, self.zsr, self.gs, self.gr) = refs
+        self.res = res
         self.n = frames // 2
         self.r, self.odd, self.me = r, lax.rem(f, 2), f // 2
         self.across = {"frame": f + 1 - 2 * self.odd}
@@ -234,22 +235,19 @@
 
         loop(1, self.n, sent)
 
-    def quarter(self, half, side):
-        return jnp.concatenate(
-            [self.res[half, side, j].astype(F32) for j in range(self.n)], axis=0
-        )
-
-
 def codec_kernel(
-    frames, refs_ref, window_ref, level_ref, x_ref, ct_ref, qs_ref, sp_ref, vp_ref, op_ref, taps_ref,
-    coded_ref, lat_ref, gs_ref, gv_ref, go_ref, gt_ref,
-    buf_ref, halo_ref, q_ref, do_ref, gp_ref, resid_ref, cth_ref, ext_ref,
-    xi_ref, k_ref, v_ref, kt_ref, vt_ref, mix_ref, dq_ref, dk_ref, dv_ref,
-    p_ref, pb_ref, inv_ref, dp_ref, ds_ref, qm_ref, dom_ref,
-    residual_ref, hx_ref, eh_ref, ph_ref, pg_ref, out_ref, rb_ref, sb_ref,
-    ssem, rsem, hs, hr, bs, br, one,
-    *sums,
+    frames, refs_ref, window_ref, level_ref, *rest,
 ):
+    inputs, rest = rest[:7], rest[7:]
+    (coded_hbm, lat_hbm, wsum_ref, psum_ref), rest = rest[:4], rest[4:]
+    held, rest = rest[:9], rest[9:]
+    x_ref, ct_ref, qs_ref, sp_ref, vp_ref, op_ref, taps_ref, coded_ref, lat_ref = held
+    (
+        buf_ref, halo_ref, q_ref, do_ref, gp_ref, resid_ref, cth_ref, ext_ref, xi_ref, k_ref,
+        v_ref, kt_ref, vt_ref, mix_ref, dq_ref, dk_ref, dv_ref, p_ref, pb_ref, inv_ref, dp_ref,
+        ds_ref, qm_ref, dom_ref, residual_ref, hx_ref, eh_ref, ph_ref, pg_ref, out_ref, rb_ref,
+        sb_ref, ssem, rsem, hs, hr, bs, br, one, local_sems,
+    ), sums = rest[:40], rest[40:]
     f = lax.axis_index("frame")
     r = lax.axis_index("row")
     tokens, width = x_ref.shape
@@ -266,9 +264,15 @@
     always = f >= 0
     partner = {"row": 1 - r}
     up, down, across = {"frame": f + 2}, {"frame": f - 2}, {"frame": pair}
-    weights = Sum(sums[:13], f, r, frames)
-    projections = Sum(sums[13:], f, r, frames)
-
+    weights = Sum(sums[:12], wsum_ref, f, r, frames)
+    projections = Sum(sums[12:], psum_ref, f, r, frames)
+
+    loads = [
+        pltpu.make_async_copy(source, target, local_sems.at[i])
+        for i, (source, target) in enumerate(zip(inputs, held))
+    ]
+    for load in loads:
+        load.start()
     barrier = pltpu.get_barrier_semaphore()
     pl.semaphore_signal(barrier, inc=1, device_id=partner, device_id_type=MESH)
     pl.semaphore_signal(barrier, inc=1, device_id=across, device_id_type=MESH)
@@ -289,9 +293,8 @@
     def place(c):
         return pl.multiple_of(jnp.where(r == 0, chunks - 1 - c, c) * step, step)
 
+    loads[0].wait()
     edge = pl.multiple_of((1 - r) * (tokens - COLS), COLS)
-    ct_copy = link(0, ct_ref.at[pl.ds(edge, COLS)], cth_ref, partner)
-    ct_copy.start()
 
     def copy(kind, c, source, device):
         part = pl.ds(place(c), step)
@@ -318,6 +321,11 @@
             copy(1, c, x_ref, down).start()
 
         copy(2, c, x_ref, across).start()
+
+    for load in loads[1:]:
+        load.wait()
+    ct_copy = link(0, ct_ref.at[pl.ds(edge, COLS)], cth_ref, partner)
+    ct_copy.start()
 
     def pass_on(c):
         @pl.when(lo2)
@@ -480,12 +488,6 @@
             dv_ref[pl.ds(at, 2 * step), :].astype(BF), vp_ref[...], 1, 1
         )
 
-    ph_ref[...] = project(
-        pl.multiple_of(jnp.where(r == 0, 2 * (tokens + rim), 0), 2 * step)
-    ).astype(BF)
-    part_copy = link(2, ph_ref, pg_ref, partner)
-    part_copy.start()
-
     sent = (hi2, lo2, always, hi4, lo4, side)
     device = (up, down, across, up, down, across)
 
@@ -508,7 +510,7 @@
                 part = jnp.where(first, block[2 * e * COLS : (2 * e + 1) * COLS], 0.0)
                 part = part + jnp.where(second, block[(2 * e + 1) * COLS : (2 * e + 2) * COLS], 0.0)
                 out_ref[kind, pl.ds(pl.multiple_of(at + e * COLS, COLS), COLS), :] = part.astype(BF)
-        for kind in (3, 4, 5, 2):
+        for kind in (3, 4, 5):
 
             @pl.when(sent[kind])
             def _():
@@ -523,6 +525,7 @@
             def _():
                 give(kind, c, out_ref.at[kind]).wait_recv()
 
+        give(2, c, out_ref.at[2]).start()
         part = pl.ds(place(c), step)
         extra = rb_ref[5, part, :].astype(F32)
         rising = out_ref[0, part, :].astype(F32) + rb_ref[3, part, :].astype(F32) + extra * even
@@ -556,11 +559,6 @@
         ).astype(BF)
 
     order = tuple(reversed(range(chunks)))
-    for c in order[:-1]:
-        hand_out(c)
-    part_copy.wait()
-    hand_out(0)
-    weights.send_totals()
     xit = xi_ref[...].T
     grad_shared = mm(x_ref[...].T, dq_ref[...]) + mm(xit, dk_ref[...].astype(BF))
     grad_values = mm(xit, dv_ref[...].astype(BF))
@@ -569,36 +567,42 @@
         projections.w[0, s] = grad_shared[s * half : (s + 1) * half]
         projections.w[1, s] = grad_values[s * half : (s + 1) * half]
     projections.begin()
+    ph_ref[...] = project(
+        pl.multiple_of(jnp.where(r == 0, 2 * (tokens + rim), 0), 2 * step)
+    ).astype(BF)
+    part_copy = link(2, ph_ref, pg_ref, partner)
+    part_copy.start()
+    hand_out(order[0])
+    projections.send_cross()
+    for c in order[1:-1]:
+        hand_out(c)
+    part_copy.wait()
+    hand_out(0)
+    weights.send_totals()
     merge(order[0])
-    projections.send_cross()
-    merge(order[1])
+    projections.send_pieces()
+    for c in order[1:-1]:
+        merge(c)
+    projections.send_totals()
+    merge(0)
     weights.send_back()
     resid_ref[...] = resid_ref[...] + mm(dq_ref[...], sp_ref[...], 1, 1)
     context = residual_ref[...]
     for t in range(3):
         context = context + mm(hx_ref[t * COLS : t * COLS + tokens, :], taps_ref[t])
     coded_ref[...] = (context * gain).astype(BF)
-    projections.send_pieces()
-    merge(order[2])
+    coded_save = pltpu.make_async_copy(coded_ref, coded_hbm, local_sems.at[7])
+    coded_save.start()
+    projections.send_back()
     weights.send_other()
-    projections.send_totals()
-    for c in order[3:]:
-        merge(c)
-    projections.send_back()
-    norm = 1.0 / math.sqrt(frames * total_rows * COLS)
-    for c in order[:2]:
+    collect(order[0])
+    projections.send_other()
+    for c in order[1:]:
         collect(c)
-    projections.send_other()
+    lat_save = pltpu.make_async_copy(lat_ref, lat_hbm, local_sems.at[8])
+    lat_save.start()
     weights.finish()
-    go_ref[...] = weights.quarter(0, 0) * norm
-    for t in range(3):
-        gt_ref[t] = weights.quarter((t + 1) // 2, (t + 1) % 2) * norm
-    for c in order[2:]:
-        collect(c)
     projections.finish()
-    for s in range(2):
-        gs_ref[s * half : (s + 1) * half, :] = projections.quarter(0, s) * norm
-        gv_ref[s * half : (s + 1) * half, :] = projections.quarter(1, s) * norm
 
     passed = (hi2, lo2, always, lo2 & hi2, lo2 & hi2, relay)
     for kind in range(KINDS):
@@ -612,6 +616,9 @@
         def _():
             for c in range(chunks):
                 give(kind, c, out_ref.at[kind]).wait_send()
+
+    coded_save.wait()
+    lat_save.wait()
 
 
 def sum_scratch(size, width, n):
@@ -624,9 +631,27 @@
         pltpu.VMEM((n, size // n, width), F32),
         pltpu.VMEM((n, size // n, width), BF),
         pltpu.VMEM((n, size // n, width), BF),
-        pltpu.VMEM((2, 2, n, size // n, width), BF),
         dma((10,)), dma((n,)), dma((n,)), dma((n,)), dma((n,)),
     ]
+
+
+def scale_kernel(
+    norm, coded_ref, lat_ref, wsum_ref, psum_ref, coded_out, lat_out, gs_ref, gv_ref, go_ref, gt_ref
+):
+    coded_out[...] = coded_ref[...]
+    lat_out[...] = lat_ref[...]
+    pieces, size = wsum_ref.shape[2:4]
+    short = psum_ref.shape[3]
+    for j in range(pieces):
+        at = slice(j * size, (j + 1) * size)
+        go_ref[at, :] = wsum_ref[0, 0, j].astype(F32) * norm
+        for t in range(3):
+            gt_ref[t, at, :] = wsum_ref[(t + 1) // 2, (t + 1) % 2, j].astype(F32) * norm
+        for side in range(2):
+            first = (side * pieces + j) * short
+            at = slice(first, first + short)
+            gs_ref[at, :] = psum_ref[0, side, j].astype(F32) * norm
+            gv_ref[at, :] = psum_ref[1, side, j].astype(F32) * norm
 
 
 def local(
@@ -643,21 +668,28 @@
     chunks = tokens // rim
     vm = pl.BlockSpec(memory_space=pltpu.VMEM)
     sm = pl.BlockSpec(memory_space=pltpu.SMEM)
+    hbm = pl.BlockSpec(memory_space=pltpu.MemorySpace.HBM)
     dma = pltpu.SemaphoreType.DMA
     slab = jax.ShapeDtypeStruct((tokens, width), BF)
     square = jax.ShapeDtypeStruct((width, width), F32)
+    pairs = frames // 2
 
     def rows_of(count, kind=BF):
         return pltpu.VMEM((count, width), kind)
 
-    coded, grad_latents, grad_shared, grad_values, grad_output, grad_taps = pl.pallas_call(
+    coded, grad_latents, weight_sum, projection_sum = pl.pallas_call(
         functools.partial(codec_kernel, frames),
         out_shape=(
-            slab, slab, square, square, square, jax.ShapeDtypeStruct((3, width, width), F32),
+            slab, slab,
+            jax.ShapeDtypeStruct((2, 2, pairs, width // pairs, width), BF),
+            jax.ShapeDtypeStruct((2, 2, pairs, width // (2 * pairs), width), BF),
         ),
-        in_specs=[sm] * 3 + [vm] * 7,
-        out_specs=(vm,) * 6,
+        in_specs=[sm] * 3 + [hbm] * 7,
+        out_specs=(hbm, hbm, vm, vm),
         scratch_shapes=[
+            rows_of(tokens), rows_of(tokens), pltpu.VMEM(quant_scale.shape, F32),
+            rows_of(width), rows_of(width), rows_of(width),
+            pltpu.VMEM(conv_taps.shape, BF), rows_of(tokens), rows_of(tokens),
             pltpu.VMEM((KINDS, tokens, width), BF),
             pltpu.VMEM((KINDS, rim, width), BF),
             rows_of(tokens), rows_of(tokens), rows_of(tokens + 4 * COLS), rows_of(tokens, F32),
@@ -679,18 +711,28 @@
             pltpu.VMEM((KINDS, tokens, width), BF),
             pltpu.VMEM((2, tokens, width), BF),
             dma((KINDS, chunks)), dma((KINDS, chunks)), dma((KINDS,)), dma((KINDS,)),
-            dma((KINDS, chunks)), dma((KINDS, chunks)), dma((6,)),
+            dma((KINDS, chunks)), dma((KINDS, chunks)), dma((6,)), dma((9,)),
         ]
         + sum_scratch(width, width, frames // 2)
         + sum_scratch(width // 2, width, frames // 2),
         compiler_params=pltpu.CompilerParams(
-            collective_id=0, has_side_effects=True, vmem_limit_bytes=62_000_000
+            collective_id=0, has_side_effects=True, vmem_limit_bytes=64_000_000
         ),
         name="codec",
     )(
         ref_frames, windows, quant_level, latents[0], cotangent[0], quant_scale,
         shared_proj, value_proj, output_proj, conv_taps,
     )
+    total = frames * lax.axis_size("row") * tokens
+    coded, grad_latents, grad_shared, grad_values, grad_output, grad_taps = pl.pallas_call(
+        functools.partial(scale_kernel, 1.0 / math.sqrt(total)),
+        out_shape=(
+            slab, slab, square, square, square, jax.ShapeDtypeStruct((3, width, width), F32),
+        ),
+        in_specs=[vm] * 4,
+        out_specs=(vm,) * 6,
+        name="scale",
+    )(coded, grad_latents, weight_sum, projection_sum)
     return (
         coded[None], grad_latents[None], grad_shared, grad_values, grad_output, grad_taps
     )

time: 72.6 us -> 64 us (0.88)
  local copies, waits for them, and re-layouts: 6.09 us -> 0 us
  Pallas kernels: 64.3 us -> 61.8 us
    unnamed x16 -> x0, local copies, waits for them, and re-layouts: 6.09 us -> none
    pallas_call x1, Pallas kernels: 64.3 us -> 59.2 us  [local(): pl.pallas_call(functools.partial(codec_kernel, frames), out_shape=(slab,...]
    pallas_call x0 -> x1, Pallas kernels: none -> 2.6 us  [local(): pl.pallas_call(functools.partial(scale_kernel, 1.0 / math.sqrt(total)), o...]
where the time goes in v3:
time: 64 us; the launch traced here: 63.8 us
  Pallas kernels  61.8 us (97%)
  between operations  1.93 us (3%)
    pallas_call x1, Pallas kernels, local(): pl.pallas_call(functools.partial(codec_kernel, frames), out_shape=(slab,...  59.2 us
    pallas_call x1, Pallas kernels, local(): pl.pallas_call(functools.partial(scale_kernel, 1.0 / math.sqrt(total)), o...  2.6 us

profile of v3, /device:TPU:0, one launch (start us, length us, event | category | flops | bytes accessed | tf_op | source)
XLA Modules:
  0.0 63.8 jit_solution(6683960562177549373)
XLA Ops:
  1.9 59.2 %codec.1 = (bf16[512,256]{1,0:T(8,128)(2,1)}, bf16[512,256]{1,0:T(8,128)(2,1)}, bf16[2,2,4,64,256]{4,3,2,1,0:T(8,128)(2,1)}, bf16[2,2,4,32,256]{4,3,2,1,0:T(8,128)(2,1)}) custom-call(s32[1,2]{1,0:T(1,128)} %refs_ref.1, s32[1]{0:T(128)S(6)} %copy.16.window_ref, s32[1]{0:T(128)S(6)} %copy.17.level_ref, bf16[512,256]{1,0:T(8,128)(2,1)} %bitcast.4, ...), custom_call_target="tpu_custom_call" | custom-call | tf_op jit(solution)/shard_map/codec/pallas_call | solution.py:680
  61.2 2.6 %scale.1 = (bf16[512,256]{1,0:T(8,128)(2,1)}, bf16[512,256]{1,0:T(8,128)(2,1)}, f32[256,256]{1,0:T(8,128)}, f32[256,256]{1,0:T(8,128)}, f32[256,256]{1,0:T(8,128)}, /*index=5*/f32[3,256,256]{2,1,0:T(8,128)}) custom-call(bf16[512,256]{1,0:T(8,128)(2,1)} %get-tuple-element.16.coded_ref, bf16[512,256]{1,0:T(8,128)(2,1)} %get-tuple-element.17.lat_ref, ...), custom_call_target="tpu_custom_call" | custom-call | tf_op jit(solution)/shard_map/scale/pallas_call | solution.py:727

commit v4 on v3

--- a/solution.py
+++ b/solution.py
@@ -13,6 +13,7 @@
 COLS = 64
 WMAX = 2
 RING = 3
+LANES = 1
 KINDS = 6
 
 SCORE_SCALE = 1.5 / math.sqrt(DH)
@@ -46,89 +47,90 @@
     return out
 
 
+def window_of(i):
+    band = 2 * COLS
+    skip = max(0, WMAX - i)
+    first = (i + skip) * band
+    return skip, first, (i + 2 * WMAX + 1) * band - first
+
+
+def features(hf):
+    return slice(hf * HALF * DH, (hf + 1) * HALF * DH)
+
+
 def forward_row(i, bias, k_ref, qm_ref, p_ref, pb_ref, inv_ref):
     band = 2 * COLS
-    reach = 2 * WMAX + 1
     wide = HALF * COLS
-    base = i * band
+    skip, first, size = window_of(i)
     kk = SCORE_SCALE * LOG2E
     for hf in range(2):
-        f0 = hf * HALF * DH
-        ft = slice(f0, f0 + HALF * DH)
-        p_ref[i, hf] = mm(k_ref[base : base + reach * band, ft], qm_ref[i, hf], 1, 1)
+        p_ref[i, hf, :size, :] = mm(k_ref[first : first + size, features(hf)], qm_ref[i, hf], 1, 1)
         m8 = None
-        for c in range(reach):
+        for c in range(size // band):
             x = p_ref[i, hf, c * band : (c + 1) * band, :].reshape(band // 8, 8, wide)
-            top = jnp.max(x, axis=0) + bias[c]
+            top = jnp.max(x, axis=0) + bias[skip + c]
             m8 = top if m8 is None else jnp.maximum(m8, top)
         m = jnp.max(m8, axis=0, keepdims=True)
         l8 = jnp.zeros((8, wide), F32)
-        for c in range(reach):
+        for c in range(size // band):
             sl = slice(c * band, (c + 1) * band)
-            p = jnp.exp2(p_ref[i, hf, sl, :] * kk + (bias[c] - m) * kk)
+            p = jnp.exp2(p_ref[i, hf, sl, :] * kk + (bias[skip + c] - m) * kk)
             p_ref[i, hf, sl, :] = p
             l8 = l8 + jnp.sum(p.reshape(band // 8, 8, wide), axis=0)
         inv = 1.0 / jnp.sum(l8, axis=0, keepdims=True)
         inv_ref[i, hf] = inv
-        for c in range(reach):
+        for c in range(size // band):
             sl = slice(c * band, (c + 1) * band)
             pb_ref[i, hf, sl, :] = (p_ref[i, hf, sl, :] * inv).astype(BF)
 
 
-def mix_row(i, vt_ref, pb_ref, mix_ref):
-    band = 2 * COLS
-    reach = 2 * WMAX + 1
-    base = i * band
+def mix_row(i, at, vt_ref, pb_ref, mix_ref):
+    _, first, size = window_of(i)
     for hf in range(2):
-        f0 = hf * HALF * DH
-        ft = slice(f0, f0 + HALF * DH)
-        mix = mm(vt_ref[ft, base : base + reach * band], pb_ref[i, hf])
-        mix_ref[i * COLS : (i + 1) * COLS, ft] = head_diagonal(mix).astype(BF)
+        ft = features(hf)
+        mix = mm(vt_ref[ft, first : first + size], pb_ref[i, hf, :size, :])
+        mix_ref[pl.ds(at, COLS), ft] = head_diagonal(mix).astype(BF)
 
 
 def score_row(i, v_ref, dom_ref, p_ref, inv_ref, dp_ref, ds_ref):
     band = 2 * COLS
-    reach = 2 * WMAX + 1
     wide = HALF * COLS
-    base = i * band
-    win = slice(base, base + reach * band)
+    slot = i % RING
+    _, first, size = window_of(i)
     for hf in range(2):
-        f0 = hf * HALF * DH
-        ft = slice(f0, f0 + HALF * DH)
-        dp_ref[i % RING, hf] = mm(v_ref[win, ft], dom_ref[i, hf], 1, 1)
+        dp_ref[slot, hf, :size, :] = mm(
+            v_ref[first : first + size, features(hf)], dom_ref[i, hf], 1, 1
+        )
         u8 = jnp.zeros((8, wide), F32)
-        for c in range(reach):
+        for c in range(size // band):
             sl = slice(c * band, (c + 1) * band)
-            x = p_ref[i, hf, sl, :] * dp_ref[i % RING, hf, sl, :]
+            x = p_ref[i, hf, sl, :] * dp_ref[slot, hf, sl, :]
             u8 = u8 + jnp.sum(x.reshape(band // 8, 8, wide), axis=0)
         inv = inv_ref[i, hf]
         ci = inv * SCORE_SCALE
         inner = jnp.sum(u8, axis=0, keepdims=True) * inv * ci
-        for c in range(reach):
+        for c in range(size // band):
             sl = slice(c * band, (c + 1) * band)
-            ds_ref[i % RING, hf, sl, :] = (p_ref[i, hf, sl, :] * (dp_ref[i % RING, hf, sl, :] * ci - inner)).astype(BF)
-
-
-def query_row(i, kt_ref, ds_ref, dq_ref):
-    band = 2 * COLS
-    base = i * band
-    win = slice(base, base + (2 * WMAX + 1) * band)
+            ds_ref[slot, hf, sl, :] = (
+                p_ref[i, hf, sl, :] * (dp_ref[slot, hf, sl, :] * ci - inner)
+            ).astype(BF)
+
+
+def query_row(i, at, kt_ref, ds_ref, dq_ref):
+    _, first, size = window_of(i)
     for hf in range(2):
-        f0 = hf * HALF * DH
-        ft = slice(f0, f0 + HALF * DH)
-        dq = mm(kt_ref[ft, win], ds_ref[i % RING, hf])
-        dq_ref[i * COLS : (i + 1) * COLS, ft] = head_diagonal(dq).astype(BF)
+        ft = features(hf)
+        dq = mm(kt_ref[ft, first : first + size], ds_ref[i % RING, hf, :size, :])
+        dq_ref[pl.ds(at, COLS), ft] = head_diagonal(dq).astype(BF)
 
 
 def key_row(i, qm_ref, dom_ref, pb_ref, ds_ref, dk_ref, dv_ref):
-    band = 2 * COLS
-    base = i * band
-    win = slice(base, base + (2 * WMAX + 1) * band)
+    _, first, size = window_of(i)
+    win = slice(first, first + size)
     for hf in range(2):
-        f0 = hf * HALF * DH
-        ft = slice(f0, f0 + HALF * DH)
-        dk_ref[win, ft] += mm(ds_ref[i % RING, hf], qm_ref[i, hf])
-        dv_ref[win, ft] += mm(pb_ref[i, hf], dom_ref[i, hf])
+        ft = features(hf)
+        dk_ref[win, ft] += mm(ds_ref[i % RING, hf, :size, :], qm_ref[i, hf])
+        dv_ref[win, ft] += mm(pb_ref[i, hf, :size, :], dom_ref[i, hf])
 
 
 def loop(first, last, body):
@@ -239,13 +241,15 @@
     frames, refs_ref, window_ref, level_ref, *rest,
 ):
     inputs, rest = rest[:7], rest[7:]
-    (coded_hbm, lat_hbm, wsum_ref, psum_ref), rest = rest[:4], rest[4:]
+    (coded_hbm, lat_hbm), totals, rest = rest[:2], rest[2 : 2 + 2 * LANES], rest[2 + 2 * LANES :]
     held, rest = rest[:9], rest[9:]
     x_ref, ct_ref, qs_ref, sp_ref, vp_ref, op_ref, taps_ref, coded_ref, lat_ref = held
+    chunks = x_ref.shape[0] // (WMAX * COLS)
+    buf_refs, rest = rest[:chunks], rest[chunks:]
     (
-        buf_ref, halo_ref, q_ref, do_ref, gp_ref, resid_ref, cth_ref, ext_ref, xi_ref, k_ref,
+        halo_ref, q_ref, do_ref, gp_ref, resid_ref, cth_ref, ext_ref, xi_ref, k_ref,
         v_ref, kt_ref, vt_ref, mix_ref, dq_ref, dk_ref, dv_ref, p_ref, pb_ref, inv_ref, dp_ref,
-        ds_ref, qm_ref, dom_ref, residual_ref, hx_ref, eh_ref, ph_ref, pg_ref, out_ref, rb_ref,
+        ds_ref, qm_ref, dom_ref, residual_ref, hx_ref, eh_ref, ph_ref, pg_ref, edge_ref, out_ref, rb_ref,
         sb_ref, ssem, rsem, hs, hr, bs, br, one, local_sems,
     ), sums = rest[:40], rest[40:]
     f = lax.axis_index("frame")
@@ -254,8 +258,10 @@
     rows = tokens // COLS
     rim = WMAX * COLS
     step = rim
-    chunks = tokens // step
-    total_rows = rows * lax.axis_size("row")
+
+    def row_at(i):
+        return pl.multiple_of(jnp.where(r == 0, i, rows - 1 - i) * COLS, COLS)
+
     odd = lax.rem(f, 2)
     pair = f + 1 - 2 * odd
     lo2, hi2, lo4, hi4 = f >= 2, f + 2 < frames, f >= 4, f + 4 < frames
@@ -264,8 +270,10 @@
     always = f >= 0
     partner = {"row": 1 - r}
     up, down, across = {"frame": f + 2}, {"frame": f - 2}, {"frame": pair}
-    weights = Sum(sums[:12], wsum_ref, f, r, frames)
-    projections = Sum(sums[12:], psum_ref, f, r, frames)
+    lanes = [
+        Sum(sums[12 * i : 12 * i + 12], totals[i], f, r, frames) for i in range(2 * LANES)
+    ]
+    weights, projections = lanes[:LANES], lanes[LANES:]
 
     loads = [
         pltpu.make_async_copy(source, target, local_sems.at[i])
@@ -297,31 +305,38 @@
     edge = pl.multiple_of((1 - r) * (tokens - COLS), COLS)
 
     def copy(kind, c, source, device):
-        part = pl.ds(place(c), step)
+        if source is x_ref:
+            source = x_ref.at[pl.ds(place(c), step)]
         return pltpu.make_async_remote_copy(
-            source.at[part], buf_ref.at[kind, part], ssem.at[kind, c], rsem.at[kind, c],
+            source, buf_refs[c].at[kind], ssem.at[kind, c], rsem.at[kind, c],
             device_id=device, device_id_type=MESH,
         )
 
     def halo(kind):
         return pltpu.make_async_remote_copy(
-            buf_ref.at[kind, pl.ds(place(0), rim)], halo_ref.at[kind], hs.at[kind], hr.at[kind],
+            buf_refs[0].at[kind], halo_ref.at[kind], hs.at[kind], hr.at[kind],
             device_id=partner, device_id_type=MESH,
         )
 
     have = (lo2, hi2, always, lo4, hi4, side)
-    for c in range(chunks):
-
-        @pl.when(hi2)
-        def _():
-            copy(0, c, x_ref, up).start()
-
-        @pl.when(lo2)
-        def _():
-            copy(1, c, x_ref, down).start()
-
-        copy(2, c, x_ref, across).start()
-
+    hops = ((0, hi2, up), (1, lo2, down), (2, always, across))
+
+    def launch(c):
+        for kind, exists, target in hops:
+
+            @pl.when(exists)
+            def _():
+                copy(kind, c, x_ref, target).start()
+
+    def launched(c):
+        for kind, exists, target in hops:
+
+            @pl.when(exists)
+            def _():
+                copy(kind, c, x_ref, target).wait_send()
+
+    launch(0)
+    launch(1)
     for load in loads[1:]:
         load.wait()
     ct_copy = link(0, ct_ref.at[pl.ds(edge, COLS)], cth_ref, partner)
@@ -336,11 +351,11 @@
 
         @pl.when(lo2 & hi2)
         def _():
-            copy(3, c, buf_ref.at[0], up).start()
+            copy(3, c, buf_refs[c].at[0], up).start()
 
         @pl.when(lo2 & (odd == 1))
         def _():
-            copy(5, c, buf_ref.at[0], across).start()
+            copy(5, c, buf_refs[c].at[0], across).start()
 
         @pl.when(hi2)
         def _():
@@ -350,11 +365,11 @@
 
         @pl.when(hi2 & lo2)
         def _():
-            copy(4, c, buf_ref.at[1], down).start()
+            copy(4, c, buf_refs[c].at[1], down).start()
 
         @pl.when(hi2 & (odd == 0))
         def _():
-            copy(5, c, buf_ref.at[1], across).start()
+            copy(5, c, buf_refs[c].at[1], across).start()
 
     level = lax.broadcasted_iota(jnp.int32, (qs_ref.shape[0], 1), 0)
     gain = jnp.sum(
@@ -377,12 +392,17 @@
         def _():
             rb_ref[kind, :, :] = jnp.zeros((tokens, width), BF)
 
+    launched(0)
+    launch(2)
     ct_copy.wait()
     outer = (cth_ref[...].astype(F32) * gain).astype(BF)
     blank = jnp.zeros_like(outer)
     ext_ref[:COLS, :] = jnp.where(r == 0, blank, outer)
     ext_ref[COLS + tokens :, :] = jnp.where(r == 0, outer, blank)
     pass_on(0)
+    for c in range(3, chunks):
+        launched(c - 2)
+        launch(c)
     resid = resid_ref[...]
     for t in range(3):
         resid = resid + mm(ext_ref[(2 - t) * COLS : (2 - t) * COLS + tokens, :], taps_ref[t], 1, 1)
@@ -391,14 +411,27 @@
     do_ref[...] = mm(resid_ref[...].astype(BF), op_ref[...], 1, 1).astype(BF)
     copy(2, 0, x_ref, across).wait_recv()
     halo(2).start()
+    for c in range(max(0, chunks - 2), chunks):
+        launched(c)
     for c in range(2, chunks):
         pass_on(c)
     for i in range(rows):
-        tok = slice(i * COLS, (i + 1) * COLS)
+        tok = pl.ds(row_at(i), COLS)
+        query, grad = q_ref[tok, :], do_ref[tok, :]
         for hf in range(2):
-            qm_ref[i, hf] = masked_rows(q_ref[tok, :], hf * HALF * DH)
-            dom_ref[i, hf] = masked_rows(do_ref[tok, :], hf * HALF * DH)
-    for c in range(chunks):
+            qm_ref[i, hf] = masked_rows(query, hf * HALF * DH)
+            dom_ref[i, hf] = masked_rows(grad, hf * HALF * DH)
+    sources = (f - 2, f + 2, pair, f - 4, f + 4, f - 1 + 2 * odd)
+    targets = (f + 2, f - 2, pair, f + 4, f - 4, f - 1 + 2 * odd)
+    kinds = []
+    for s in range(2):
+        own = refs_ref[0, s]
+        kind = jnp.int32(0)
+        for number, source in enumerate(sources):
+            kind = jnp.where(own == source, number, kind)
+        kinds.append(kind)
+
+    def arrive(c):
         for kind in range(2, KINDS):
             if kind > 2 or c:
 
@@ -408,59 +441,76 @@
                     if c == 0:
                         halo(kind).start()
 
+    def take(first, piece):
+        for d in range(WMAX):
+            for s in range(2):
+                at = (2 * (first + d) + s) * COLS
+                xi_ref[at : at + COLS, :] = piece(s, d)
+        part = slice(2 * first * COLS, 2 * (first + WMAX) * COLS)
+        keys = mm(xi_ref[part, :], sp_ref[...]).astype(BF)
+        k_ref[part, :] = keys
+        kt_ref[:, part] = keys.T
+        vals = mm(xi_ref[part, :], vp_ref[...]).astype(BF)
+        v_ref[part, :] = vals
+        vt_ref[:, part] = vals.T
+
+    def sub(d):
+        return pl.ds(pl.multiple_of(jnp.where(r == 0, d, 1 - d) * COLS, COLS), COLS)
+
+    def take_chunk(c):
+        take(WMAX + rows - WMAX * (c + 1), lambda s, d: buf_refs[c][kinds[s], sub(d), :])
+
+    window = window_ref[0]
+    bias = [
+        jnp.where(abs(c - WMAX) <= window, 0.0, -jnp.inf).astype(F32) for c in range(2 * WMAX + 1)
+    ]
+
+    def forward(last, first):
+        for i in range(last, first - 1, -1):
+            forward_row(i, bias, k_ref, qm_ref, p_ref, pb_ref, inv_ref)
+
+    def mix(last, first):
+        for i in range(last, first - 1, -1):
+            mix_row(i, row_at(i), vt_ref, pb_ref, mix_ref)
+
+    arrive(0)
+    arrive(1)
+    take_chunk(0)
+    take_chunk(1)
     for kind in range(KINDS):
 
         @pl.when(have[kind])
         def _():
             halo(kind).wait()
 
-    sources = (f - 2, f + 2, pair, f - 4, f + 4, f - 1 + 2 * odd)
-    targets = (f + 2, f - 2, pair, f + 4, f - 4, f - 1 + 2 * odd)
-    for s in range(2):
-        own = refs_ref[0, s]
-        kind = jnp.int32(0)
-        for number, source in enumerate(sources):
-            kind = jnp.where(own == source, number, kind)
-        for e in range(rows):
-            at = (2 * (e + WMAX) + s) * COLS
-            xi_ref[at : at + COLS, :] = buf_ref[kind, e * COLS : (e + 1) * COLS, :]
-        for e in range(WMAX):
-            piece = halo_ref[kind, e * COLS : (e + 1) * COLS, :]
-            none = jnp.zeros_like(piece)
-            at = (2 * e + s) * COLS
-            xi_ref[at : at + COLS, :] = jnp.where(r == 0, none, piece)
-            at = (2 * (e + WMAX + rows) + s) * COLS
-            xi_ref[at : at + COLS, :] = jnp.where(r == 0, piece, none)
-
-    keys = mm(xi_ref[...], sp_ref[...]).astype(BF)
-    k_ref[...] = keys
-    kt_ref[...] = keys.T
-    vals = mm(xi_ref[...], vp_ref[...]).astype(BF)
-    v_ref[...] = vals
-    vt_ref[...] = vals.T
-    first_row = r * rows
-    window = window_ref[0]
-
-    def bias_of(i):
-        out = []
-        for c in range(2 * WMAX + 1):
-            key_row = first_row + i + c - WMAX
-            inside = (key_row >= 0) & (key_row < total_rows) & (abs(c - WMAX) <= window)
-            out.append(jnp.where(inside, 0.0, -jnp.inf).astype(F32))
-        return out
-
-    for i in range(rows):
-        forward_row(i, bias_of(i), k_ref, qm_ref, p_ref, pb_ref, inv_ref)
-    for i in range(rows):
-        mix_row(i, vt_ref, pb_ref, mix_ref)
+    take(WMAX + rows, lambda s, d: halo_ref[kinds[s], sub(d), :])
+    low = rows - WMAX
+    forward(rows - 1, low)
+    mix(rows - 1, low)
+    inner = row_at(rows - 1)
+    edge_ref[...] = (
+        x_ref[pl.ds(inner, COLS), :].astype(F32) + mm(mix_ref[pl.ds(inner, COLS), :], op_ref[...])
+    ).astype(BF)
+    hidden_copy = link(1, edge_ref, eh_ref, partner)
+    hidden_copy.start()
+    for c in range(2, chunks):
+        arrive(c)
+        take_chunk(c)
+        below = low - WMAX if c < chunks - 1 else 0
+        forward(low - 1, below)
+        mix(low - 1, below)
+        low = below
 
     residual = x_ref[...].astype(F32) + mm(mix_ref[...], op_ref[...])
     residual_ref[...] = residual
     hx_ref[COLS : COLS + tokens, :] = residual.astype(BF)
-    inner = pl.multiple_of(COLS + (1 - r) * (tokens - COLS), COLS)
-    hidden_copy = link(1, hx_ref.at[pl.ds(inner, COLS)], eh_ref, partner)
-    hidden_copy.start()
-    weights.w[0, 0] = mm(mix_ref[...].T, resid_ref[...].astype(BF))
+
+    def fill(half, side, value):
+        size = width // LANES
+        for i, lane in enumerate(weights):
+            lane.w[half, side] = value[i * size : (i + 1) * size]
+
+    fill(0, 0, mm(mix_ref[...].T, resid_ref[...].astype(BF)))
     hidden_copy.wait()
     outer = eh_ref[...]
     blank = jnp.zeros_like(outer)
@@ -469,25 +519,17 @@
     hxt = hx_ref[...].T
     span = tokens + 2 * COLS
     for t in range(3):
-        weights.w[(t + 1) // 2, (t + 1) % 2] = mm(hxt, gp_ref[(2 - t) * COLS : (2 - t) * COLS + span, :])
-    weights.begin()
-
-    for i in range(rows + 1):
-        if i == 2:
-            weights.send_cross()
-        if i == 6:
-            weights.send_pieces()
-        if i < rows:
-            score_row(i, v_ref, dom_ref, p_ref, inv_ref, dp_ref, ds_ref)
-        if i:
-            key_row(i - 1, qm_ref, dom_ref, pb_ref, ds_ref, dk_ref, dv_ref)
-            query_row(i - 1, kt_ref, ds_ref, dq_ref)
-
-    def project(at):
-        return mm(dk_ref[pl.ds(at, 2 * step), :].astype(BF), sp_ref[...], 1, 1) + mm(
-            dv_ref[pl.ds(at, 2 * step), :].astype(BF), vp_ref[...], 1, 1
-        )
-
+        fill((t + 1) // 2, (t + 1) % 2, mm(hxt, gp_ref[(2 - t) * COLS : (2 - t) * COLS + span, :]))
+    for lane in weights:
+        lane.begin()
+
+    def project(first):
+        part = slice(2 * first * COLS, 2 * (first + WMAX) * COLS)
+        return mm(dk_ref[part, :].astype(BF), sp_ref[...], 1, 1) + mm(
+            dv_ref[part, :].astype(BF), vp_ref[...], 1, 1
+        )
+
+    part_copy = link(2, ph_ref, pg_ref, partner)
     sent = (hi2, lo2, always, hi4, lo4, side)
     device = (up, down, across, up, down, across)
 
@@ -499,17 +541,18 @@
         )
 
     def hand_out(c):
-        at = place(c)
-        block = project(pl.multiple_of(2 * at + 2 * rim, 2 * step))
+        first = rows - WMAX * (c + 1)
+        block = project(WMAX + first)
         if c == 0:
-            block = block + pg_ref[...].astype(F32)
+            band = 2 * COLS
+            block = block + jnp.concatenate([pg_ref[band:, :], pg_ref[:band, :]], axis=0).astype(F32)
         for kind, target in enumerate(targets):
-            first = refs_ref[0, 0] == target
-            second = refs_ref[0, 1] == target
-            for e in range(WMAX):
-                part = jnp.where(first, block[2 * e * COLS : (2 * e + 1) * COLS], 0.0)
-                part = part + jnp.where(second, block[(2 * e + 1) * COLS : (2 * e + 2) * COLS], 0.0)
-                out_ref[kind, pl.ds(pl.multiple_of(at + e * COLS, COLS), COLS), :] = part.astype(BF)
+            one_is = refs_ref[0, 0] == target
+            two_is = refs_ref[0, 1] == target
+            for d in range(WMAX):
+                part = jnp.where(one_is, block[2 * d * COLS : (2 * d + 1) * COLS], 0.0)
+                part = part + jnp.where(two_is, block[(2 * d + 1) * COLS : (2 * d + 2) * COLS], 0.0)
+                out_ref[kind, pl.ds(row_at(first + d), COLS), :] = part.astype(BF)
         for kind in (3, 4, 5):
 
             @pl.when(sent[kind])
@@ -558,34 +601,57 @@
             + rb_ref[2, part, :].astype(F32)
         ).astype(BF)
 
-    order = tuple(reversed(range(chunks)))
-    xit = xi_ref[...].T
-    grad_shared = mm(x_ref[...].T, dq_ref[...]) + mm(xit, dk_ref[...].astype(BF))
-    grad_values = mm(xit, dv_ref[...].astype(BF))
-    half = width // 2
-    for s in range(2):
-        projections.w[0, s] = grad_shared[s * half : (s + 1) * half]
-        projections.w[1, s] = grad_values[s * half : (s + 1) * half]
-    projections.begin()
-    ph_ref[...] = project(
-        pl.multiple_of(jnp.where(r == 0, 2 * (tokens + rim), 0), 2 * step)
-    ).astype(BF)
-    part_copy = link(2, ph_ref, pg_ref, partner)
-    part_copy.start()
-    hand_out(order[0])
-    projections.send_cross()
-    for c in order[1:-1]:
-        hand_out(c)
-    part_copy.wait()
-    hand_out(0)
-    weights.send_totals()
-    merge(order[0])
-    projections.send_pieces()
-    for c in order[1:-1]:
-        merge(c)
-    projections.send_totals()
+    for t in range(rows + 1):
+        i = rows - 1 - t
+        if t == 2:
+            for lane in weights:
+                lane.send_cross()
+        if t > rows - 3 and t - (rows - 2) < LANES:
+            weights[t - (rows - 2)].send_pieces()
+        if t < rows:
+            score_row(i, v_ref, dom_ref, p_ref, inv_ref, dp_ref, ds_ref)
+        if t:
+            key_row(i + 1, qm_ref, dom_ref, pb_ref, ds_ref, dk_ref, dv_ref)
+            query_row(i + 1, row_at(i + 1), kt_ref, ds_ref, dq_ref)
+        if t == WMAX:
+            ph_ref[...] = project(WMAX + rows).astype(BF)
+            part_copy.start()
+        if t == 2 * WMAX:
+            part_copy.wait()
+            hand_out(0)
+        if t > 2 * WMAX and t % WMAX == 0 and t < rows:
+            hand_out(t // WMAX - WMAX)
+    inside = 2 * WMAX * COLS
+    xit = xi_ref[inside:, :].T
+    grad_shared = mm(x_ref[...].T, dq_ref[...]) + mm(xit, dk_ref[inside:, :].astype(BF))
+    grad_values = mm(xit, dv_ref[inside:, :].astype(BF))
+    short = width // (2 * LANES)
+    for i, lane in enumerate(projections):
+        for side_ in range(2):
+            part = slice((2 * i + side_) * short, (2 * i + side_ + 1) * short)
+            lane.w[0, side_] = grad_shared[part]
+            lane.w[1, side_] = grad_values[part]
+        lane.begin()
+    hand_out(2)
+    hand_out(3)
+    for lane in projections:
+        lane.send_cross()
+    for lane in weights:
+        lane.send_totals()
+    for lane in projections:
+        lane.send_pieces()
     merge(0)
-    weights.send_back()
+    merge(1)
+    for lane in projections:
+        lane.send_totals()
+    for lane in weights:
+        lane.send_back()
+    merge(2)
+    merge(3)
+    for lane in projections:
+        lane.send_back()
+    for lane in weights:
+        lane.send_other()
     resid_ref[...] = resid_ref[...] + mm(dq_ref[...], sp_ref[...], 1, 1)
     context = residual_ref[...]
     for t in range(3):
@@ -593,24 +659,25 @@
     coded_ref[...] = (context * gain).astype(BF)
     coded_save = pltpu.make_async_copy(coded_ref, coded_hbm, local_sems.at[7])
     coded_save.start()
-    projections.send_back()
-    weights.send_other()
-    collect(order[0])
-    projections.send_other()
-    for c in order[1:]:
-        collect(c)
+    for lane in projections:
+        lane.send_other()
+    collect(0)
+    collect(1)
+    collect(2)
+    collect(3)
     lat_save = pltpu.make_async_copy(lat_ref, lat_hbm, local_sems.at[8])
     lat_save.start()
-    weights.finish()
-    projections.finish()
-
-    passed = (hi2, lo2, always, lo2 & hi2, lo2 & hi2, relay)
+    for lane in lanes:
+        lane.finish()
+
     for kind in range(KINDS):
 
-        @pl.when(passed[kind])
-        def _():
-            for c in range(chunks):
-                copy(kind, c, x_ref, across).wait_send()
+        if kind > 2:
+
+            @pl.when(got[kind])
+            def _():
+                for c in range(chunks):
+                    copy(kind, c, x_ref, across).wait_send()
 
         @pl.when(sent[kind])
         def _():
@@ -635,23 +702,24 @@
     ]
 
 
-def scale_kernel(
-    norm, coded_ref, lat_ref, wsum_ref, psum_ref, coded_out, lat_out, gs_ref, gv_ref, go_ref, gt_ref
-):
+def scale_kernel(norm, coded_ref, lat_ref, *rest):
+    totals = rest[: 2 * LANES]
+    coded_out, lat_out, gs_ref, gv_ref, go_ref, gt_ref = rest[2 * LANES :]
     coded_out[...] = coded_ref[...]
     lat_out[...] = lat_ref[...]
-    pieces, size = wsum_ref.shape[2:4]
-    short = psum_ref.shape[3]
-    for j in range(pieces):
-        at = slice(j * size, (j + 1) * size)
-        go_ref[at, :] = wsum_ref[0, 0, j].astype(F32) * norm
-        for t in range(3):
-            gt_ref[t, at, :] = wsum_ref[(t + 1) // 2, (t + 1) % 2, j].astype(F32) * norm
-        for side in range(2):
-            first = (side * pieces + j) * short
-            at = slice(first, first + short)
-            gs_ref[at, :] = psum_ref[0, side, j].astype(F32) * norm
-            gv_ref[at, :] = psum_ref[1, side, j].astype(F32) * norm
+    for i in range(LANES):
+        large, small = totals[i], totals[LANES + i]
+        pieces, size = large.shape[2:4]
+        short = small.shape[3]
+        for j in range(pieces):
+            at = pl.ds((i * pieces + j) * size, size)
+            go_ref[at, :] = large[0, 0, j].astype(F32) * norm
+            for t in range(3):
+                gt_ref[t, at, :] = large[(t + 1) // 2, (t + 1) % 2, j].astype(F32) * norm
+            for side in range(2):
+                at = pl.ds(((2 * i + side) * pieces + j) * short, short)
+                gs_ref[at, :] = small[0, side, j].astype(F32) * norm
+                gv_ref[at, :] = small[1, side, j].astype(F32) * norm
 
 
 def local(
@@ -673,25 +741,28 @@
     slab = jax.ShapeDtypeStruct((tokens, width), BF)
     square = jax.ShapeDtypeStruct((width, width), F32)
     pairs = frames // 2
+    sizes = (width // LANES,) * LANES + (width // (2 * LANES),) * LANES
 
     def rows_of(count, kind=BF):
         return pltpu.VMEM((count, width), kind)
 
-    coded, grad_latents, weight_sum, projection_sum = pl.pallas_call(
+    coded, grad_latents, *totals = pl.pallas_call(
         functools.partial(codec_kernel, frames),
         out_shape=(
             slab, slab,
-            jax.ShapeDtypeStruct((2, 2, pairs, width // pairs, width), BF),
-            jax.ShapeDtypeStruct((2, 2, pairs, width // (2 * pairs), width), BF),
+        )
+        + tuple(
+            jax.ShapeDtypeStruct((2, 2, pairs, size // pairs, width), BF) for size in sizes
         ),
         in_specs=[sm] * 3 + [hbm] * 7,
-        out_specs=(hbm, hbm, vm, vm),
+        out_specs=(hbm, hbm) + (vm,) * (2 * LANES),
         scratch_shapes=[
             rows_of(tokens), rows_of(tokens), pltpu.VMEM(quant_scale.shape, F32),
             rows_of(width), rows_of(width), rows_of(width),
             pltpu.VMEM(conv_taps.shape, BF), rows_of(tokens), rows_of(tokens),
-            pltpu.VMEM((KINDS, tokens, width), BF),
-            pltpu.VMEM((KINDS, rim, width), BF),
+        ]
+        + [pltpu.VMEM((KINDS, rim, width), BF)] * (chunks + 1)
+        + [
             rows_of(tokens), rows_of(tokens), rows_of(tokens + 4 * COLS), rows_of(tokens, F32),
             rows_of(COLS), rows_of(tokens + 2 * COLS),
             rows_of(2 * ext), rows_of(2 * ext), rows_of(2 * ext),
@@ -706,15 +777,14 @@
             pltpu.VMEM((rows, 2, wide, HALF * DH), BF),
             pltpu.VMEM((rows, 2, wide, HALF * DH), BF),
             rows_of(tokens, F32), rows_of(tokens + 2 * COLS), rows_of(COLS),
-            rows_of(2 * rim), rows_of(2 * rim),
+            rows_of(2 * rim), rows_of(2 * rim), rows_of(COLS),
             pltpu.VMEM((KINDS, tokens, width), BF),
             pltpu.VMEM((KINDS, tokens, width), BF),
             pltpu.VMEM((2, tokens, width), BF),
             dma((KINDS, chunks)), dma((KINDS, chunks)), dma((KINDS,)), dma((KINDS,)),
             dma((KINDS, chunks)), dma((KINDS, chunks)), dma((6,)), dma((9,)),
         ]
-        + sum_scratch(width, width, frames // 2)
-        + sum_scratch(width // 2, width, frames // 2),
+        + [ref for size in sizes for ref in sum_scratch(size, width, pairs)],
         compiler_params=pltpu.CompilerParams(
             collective_id=0, has_side_effects=True, vmem_limit_bytes=64_000_000
         ),
@@ -729,10 +799,10 @@
         out_shape=(
             slab, slab, square, square, square, jax.ShapeDtypeStruct((3, width, width), F32),
         ),
-        in_specs=[vm] * 4,
+        in_specs=[vm] * (2 + 2 * LANES),
         out_specs=(vm,) * 6,
         name="scale",
-    )(coded, grad_latents, weight_sum, projection_sum)
+    )(coded, grad_latents, *totals)
     return (
         coded[None], grad_latents[None], grad_shared, grad_values, grad_output, grad_taps
     )

time: 64 us -> 61.1 us (0.955)
  Pallas kernels: 61.8 us -> 58.9 us
    pallas_call x1, Pallas kernels: 59.2 us -> 56.4 us  [local(): pl.pallas_call(functools.partial(codec_kernel, frames), out_shape=(slab,...]
where the time goes in v4:
time: 61.1 us; the launch traced here: 60.9 us
  Pallas kernels  58.9 us (96%)
  between operations  1.93 us (3%)
    pallas_call x1, Pallas kernels, local(): pl.pallas_call(functools.partial(codec_kernel, frames), out_shape=(slab,...  56.4 us
    pallas_call x1, Pallas kernels, local(): pl.pallas_call(functools.partial(scale_kernel, 1.0 / math.sqrt(total)), o...  2.6 us

profile of v4, /device:TPU:0, one launch (start us, length us, event | category | flops | bytes accessed | tf_op | source)
XLA Modules:
  0.0 60.9 jit_solution(12596910640389075108)
XLA Ops:
  1.9 56.4 %codec.1 = (bf16[512,256]{1,0:T(8,128)(2,1)}, bf16[512,256]{1,0:T(8,128)(2,1)}, bf16[2,2,4,64,256]{4,3,2,1,0:T(8,128)(2,1)}, bf16[2,2,4,32,256]{4,3,2,1,0:T(8,128)(2,1)}) custom-call(s32[1,2]{1,0:T(1,128)} %refs_ref.1, s32[1]{0:T(128)S(6)} %copy.16.window_ref, s32[1]{0:T(128)S(6)} %copy.17.level_ref, bf16[512,256]{1,0:T(8,128)(2,1)} %bitcast.4, ...), custom_call_target="tpu_custom_call" | custom-call | tf_op jit(solution)/shard_map/codec/pallas_call | solution.py:749
  58.3 2.6 %scale.1 = (bf16[512,256]{1,0:T(8,128)(2,1)}, bf16[512,256]{1,0:T(8,128)(2,1)}, f32[256,256]{1,0:T(8,128)}, f32[256,256]{1,0:T(8,128)}, f32[256,256]{1,0:T(8,128)}, /*index=5*/f32[3,256,256]{2,1,0:T(8,128)}) custom-call(bf16[512,256]{1,0:T(8,128)(2,1)} %get-tuple-element.16.coded_ref, bf16[512,256]{1,0:T(8,128)(2,1)} %get-tuple-element.17.lat_ref, ...), custom_call_target="tpu_custom_call" | custom-call | tf_op jit(solution)/shard_map/scale/pallas_call | solution.py:797

commit v5 on v4

--- a/solution.py
+++ b/solution.py
@@ -473,56 +473,6 @@
         for i in range(last, first - 1, -1):
             mix_row(i, row_at(i), vt_ref, pb_ref, mix_ref)
 
-    arrive(0)
-    arrive(1)
-    take_chunk(0)
-    take_chunk(1)
-    for kind in range(KINDS):
-
-        @pl.when(have[kind])
-        def _():
-            halo(kind).wait()
-
-    take(WMAX + rows, lambda s, d: halo_ref[kinds[s], sub(d), :])
-    low = rows - WMAX
-    forward(rows - 1, low)
-    mix(rows - 1, low)
-    inner = row_at(rows - 1)
-    edge_ref[...] = (
-        x_ref[pl.ds(inner, COLS), :].astype(F32) + mm(mix_ref[pl.ds(inner, COLS), :], op_ref[...])
-    ).astype(BF)
-    hidden_copy = link(1, edge_ref, eh_ref, partner)
-    hidden_copy.start()
-    for c in range(2, chunks):
-        arrive(c)
-        take_chunk(c)
-        below = low - WMAX if c < chunks - 1 else 0
-        forward(low - 1, below)
-        mix(low - 1, below)
-        low = below
-
-    residual = x_ref[...].astype(F32) + mm(mix_ref[...], op_ref[...])
-    residual_ref[...] = residual
-    hx_ref[COLS : COLS + tokens, :] = residual.astype(BF)
-
-    def fill(half, side, value):
-        size = width // LANES
-        for i, lane in enumerate(weights):
-            lane.w[half, side] = value[i * size : (i + 1) * size]
-
-    fill(0, 0, mm(mix_ref[...].T, resid_ref[...].astype(BF)))
-    hidden_copy.wait()
-    outer = eh_ref[...]
-    blank = jnp.zeros_like(outer)
-    hx_ref[:COLS, :] = jnp.where(r == 0, blank, outer)
-    hx_ref[COLS + tokens :, :] = jnp.where(r == 0, outer, blank)
-    hxt = hx_ref[...].T
-    span = tokens + 2 * COLS
-    for t in range(3):
-        fill((t + 1) // 2, (t + 1) % 2, mm(hxt, gp_ref[(2 - t) * COLS : (2 - t) * COLS + span, :]))
-    for lane in weights:
-        lane.begin()
-
     def project(first):
         part = slice(2 * first * COLS, 2 * (first + WMAX) * COLS)
         return mm(dk_ref[part, :].astype(BF), sp_ref[...], 1, 1) + mm(
@@ -601,26 +551,78 @@
             + rb_ref[2, part, :].astype(F32)
         ).astype(BF)
 
-    for t in range(rows + 1):
-        i = rows - 1 - t
-        if t == 2:
-            for lane in weights:
-                lane.send_cross()
-        if t > rows - 3 and t - (rows - 2) < LANES:
-            weights[t - (rows - 2)].send_pieces()
-        if t < rows:
+    def finish_forward():
+        residual = x_ref[...].astype(F32) + mm(mix_ref[...], op_ref[...])
+        residual_ref[...] = residual
+        hx_ref[COLS : COLS + tokens, :] = residual.astype(BF)
+
+        def fill(half, side, value):
+            size = width // LANES
+            for i, lane in enumerate(weights):
+                lane.w[half, side] = value[i * size : (i + 1) * size]
+
+        fill(0, 0, mm(mix_ref[...].T, resid_ref[...].astype(BF)))
+        hidden_copy.wait()
+        outer = eh_ref[...]
+        blank = jnp.zeros_like(outer)
+        hx_ref[:COLS, :] = jnp.where(r == 0, blank, outer)
+        hx_ref[COLS + tokens :, :] = jnp.where(r == 0, outer, blank)
+        hxt = hx_ref[...].T
+        span = tokens + 2 * COLS
+        for t in range(3):
+            fill((t + 1) // 2, (t + 1) % 2, mm(hxt, gp_ref[(2 - t) * COLS : (2 - t) * COLS + span, :]))
+        for lane in weights:
+            lane.begin()
+
+    def back(last, first):
+        for i in range(last, first - 1, -1):
             score_row(i, v_ref, dom_ref, p_ref, inv_ref, dp_ref, ds_ref)
-        if t:
-            key_row(i + 1, qm_ref, dom_ref, pb_ref, ds_ref, dk_ref, dv_ref)
-            query_row(i + 1, row_at(i + 1), kt_ref, ds_ref, dq_ref)
-        if t == WMAX:
-            ph_ref[...] = project(WMAX + rows).astype(BF)
-            part_copy.start()
-        if t == 2 * WMAX:
-            part_copy.wait()
-            hand_out(0)
-        if t > 2 * WMAX and t % WMAX == 0 and t < rows:
-            hand_out(t // WMAX - WMAX)
+        for i in range(last, first - 1, -1):
+            key_row(i, qm_ref, dom_ref, pb_ref, ds_ref, dk_ref, dv_ref)
+            query_row(i, row_at(i), kt_ref, ds_ref, dq_ref)
+
+    arrive(0)
+    arrive(1)
+    take_chunk(0)
+    take_chunk(1)
+    for kind in range(KINDS):
+
+        @pl.when(have[kind])
+        def _():
+            halo(kind).wait()
+
+    take(WMAX + rows, lambda s, d: halo_ref[kinds[s], sub(d), :])
+    low = rows - WMAX
+    forward(rows - 1, low)
+    mix(rows - 1, low)
+    inner = row_at(rows - 1)
+    edge_ref[...] = (
+        x_ref[pl.ds(inner, COLS), :].astype(F32) + mm(mix_ref[pl.ds(inner, COLS), :], op_ref[...])
+    ).astype(BF)
+    hidden_copy = link(1, edge_ref, eh_ref, partner)
+    hidden_copy.start()
+    back(rows - 1, low)
+    ph_ref[...] = project(WMAX + rows).astype(BF)
+    part_copy.start()
+    for c in range(2, chunks):
+        arrive(c)
+        take_chunk(c)
+        below = low - WMAX if c < chunks - 1 else 0
+        forward(low - 1, below)
+        mix(low - 1, below)
+        if c == chunks - 1:
+            finish_forward()
+        for top in range(low, below, -WMAX):
+            back(top - 1, top - WMAX)
+            done = (rows - top) // WMAX - 1
+            if done == 0:
+                part_copy.wait()
+            if done < chunks - WMAX:
+                hand_out(done)
+            if c == chunks - 1 and done == 1:
+                for lane in weights:
+                    lane.send_cross()
+        low = below
     inside = 2 * WMAX * COLS
     xit = xi_ref[inside:, :].T
     grad_shared = mm(x_ref[...].T, dq_ref[...]) + mm(xit, dk_ref[inside:, :].astype(BF))
@@ -632,26 +634,22 @@
             lane.w[0, side_] = grad_shared[part]
             lane.w[1, side_] = grad_values[part]
         lane.begin()
-    hand_out(2)
-    hand_out(3)
+    hand_out(chunks - 2)
+    hand_out(chunks - 1)
     for lane in projections:
         lane.send_cross()
     for lane in weights:
+        lane.send_pieces()
+    merge(0)
+    for lane in projections:
+        lane.send_pieces()
+    merge(1)
+    for lane in weights:
         lane.send_totals()
     for lane in projections:
-        lane.send_pieces()
-    merge(0)
-    merge(1)
-    for lane in projections:
         lane.send_totals()
-    for lane in weights:
-        lane.send_back()
     merge(2)
     merge(3)
-    for lane in projections:
-        lane.send_back()
-    for lane in weights:
-        lane.send_other()
     resid_ref[...] = resid_ref[...] + mm(dq_ref[...], sp_ref[...], 1, 1)
     context = residual_ref[...]
     for t in range(3):
@@ -659,12 +657,17 @@
     coded_ref[...] = (context * gain).astype(BF)
     coded_save = pltpu.make_async_copy(coded_ref, coded_hbm, local_sems.at[7])
     coded_save.start()
+    for lane in weights:
+        lane.send_back()
+    for lane in projections:
+        lane.send_back()
+    collect(0)
+    for lane in weights:
+        lane.send_other()
     for lane in projections:
         lane.send_other()
-    collect(0)
-    collect(1)
-    collect(2)
-    collect(3)
+    for c in range(1, chunks):
+        collect(c)
     lat_save = pltpu.make_async_copy(lat_ref, lat_hbm, local_sems.at[8])
     lat_save.start()
     for lane in lanes:

time: 61.1 us -> 60.9 us (level)
  no operation moved by 1% of the time
where the time goes in v5:
time: 60.9 us; the launch traced here: 60.7 us
  Pallas kernels  58.8 us (97%)
  between operations  1.93 us (3%)
    pallas_call x1, Pallas kernels, local(): pl.pallas_call(functools.partial(codec_kernel, frames), out_shape=(slab,...  56.2 us
    pallas_call x1, Pallas kernels, local(): pl.pallas_call(functools.partial(scale_kernel, 1.0 / math.sqrt(total)), o...  2.6 us

profile of v5, /device:TPU:0, one launch (start us, length us, event | category | flops | bytes accessed | tf_op | source)
XLA Modules:
  0.0 60.7 jit_solution(10531176243681771011)
XLA Ops:
  1.9 56.2 %codec.1 = (bf16[512,256]{1,0:T(8,128)(2,1)}, bf16[512,256]{1,0:T(8,128)(2,1)}, bf16[2,2,4,64,256]{4,3,2,1,0:T(8,128)(2,1)}, bf16[2,2,4,32,256]{4,3,2,1,0:T(8,128)(2,1)}) custom-call(s32[1,2]{1,0:T(1,128)} %refs_ref.1, s32[1]{0:T(128)S(6)} %copy.16.window_ref, s32[1]{0:T(128)S(6)} %copy.17.level_ref, bf16[512,256]{1,0:T(8,128)(2,1)} %bitcast.4, ...), custom_call_target="tpu_custom_call" | custom-call | tf_op jit(solution)/shard_map/codec/pallas_call | solution.py:752
  58.1 2.6 %scale.1 = (bf16[512,256]{1,0:T(8,128)(2,1)}, bf16[512,256]{1,0:T(8,128)(2,1)}, f32[256,256]{1,0:T(8,128)}, f32[256,256]{1,0:T(8,128)}, f32[256,256]{1,0:T(8,128)}, /*index=5*/f32[3,256,256]{2,1,0:T(8,128)}) custom-call(bf16[512,256]{1,0:T(8,128)(2,1)} %get-tuple-element.16.coded_ref, bf16[512,256]{1,0:T(8,128)(2,1)} %get-tuple-element.17.lat_ref, ...), custom_call_target="tpu_custom_call" | custom-call | tf_op jit(solution)/shard_map/scale/pallas_call | solution.py:800
